TPU v7x, 32 devices: a whole 2x2x4 slice. The times are simulated.
32 devices in a mesh: wide: 8 (over z, x), chol: 4 (over y, core).
Axes of the slice: x: 2, y: 2, z: 4, core: 2. Of those that a mesh axis runs over, the one named last changes fastest.
Arguments:
- walkers: bfloat16 [8, 2048, 256], P('wide', 'chol'), may hold values from -6 to 6
- intersection_inv: bfloat16 [8, 256, 256], P('wide'), may hold values from -0.375 to 0.375
- trial_state: bfloat16 [2048, 256], replicated, may hold values from -0.125 to 0.125
- chol_tiles: bfloat16 [2048, 128, 128], P(('wide', 'chol')), may hold values from -1.25 to 1.25
- tile_vector: int32 [2048], P(('wide', 'chol')), may hold values from 0 to 63
- tile_row: int32 [2048], P(('wide', 'chol')), may hold values from 0 to 15
- tile_col: int32 [2048], P(('wide', 'chol')), may hold values from 0 to 3
- tile_count: int32 [32], P(('wide', 'chol')), may hold values from 32 to 64, as said below
- sources: int32 [8], replicated, may hold values from 0 to 7
- aux_noise: float32 [8, 512], P(None, 'wide'), may hold values from -6 to 6
Outputs:
- force_bias: float32 [8, 512], P(None, 'wide')
- new_walkers: bfloat16 [8, 2048, 256], P('wide', 'chol')
Inputs may be any that keep to these rules, and one draw needn't show every extreme that they name: `tile_count`: slots beyond a device's count are ignored; some device has all 64 slots live.
All inputs are finite; a program needn't handle non-finite values.
Results may differ from a plain program's by a relative error of at most 0.019.
Values may be sent and summed in bfloat16 or wider, within the bound.
A program may use at most 192 MiB of HBM per device.

v0:
```python
import jax
import jax.numpy as jnp
from jax import lax
from jax.sharding import PartitionSpec as P

TAYLOR = 4


SQRT_TAU = 0.1


def body(
    walkers,
    intersection_inv,
    trial_state,
    chol_tiles,
    tile_vector,
    tile_row,
    tile_col,
    tile_count,
    sources,
    aux_noise,
):
    f32 = jnp.float32
    bf16 = jnp.bfloat16
    highest = lax.Precision.HIGHEST
    walk_dev, orb_rows, electrons = walkers.shape
    slot_count, tile_size, _ = chol_tiles.shape
    orbitals = trial_state.shape[0]
    row_blocks = orbitals // tile_size
    col_blocks = orb_rows // tile_size
    walk_all, vec_dev = aux_noise.shape
    theta_own = jnp.einsum(
        "wmn,wnk->wmk", walkers, intersection_inv, preferred_element_type=f32
    ).astype(bf16)
    walker_rows, theta_all = (
        lax.all_gather(walkers, "wide", axis=0, tiled=True),
        lax.all_gather(theta_own, "wide", axis=0, tiled=True),
    )
    picker = (sources[:, None] == jnp.arange(walk_all, dtype=jnp.int32)[None, :]).astype(bf16)
    theta_new = jnp.einsum("jw,wmn->jmn", picker, theta_all, preferred_element_type=f32).astype(
        bf16
    )
    own_pick = lax.dynamic_slice_in_dim(picker, lax.axis_index("wide") * walk_dev, walk_dev, 0)
    own_walkers = jnp.einsum(
        "jw,wmn->jmn", own_pick, walker_rows, preferred_element_type=f32
    ).astype(bf16)
    row_hot = (tile_row[:, None] == jnp.arange(row_blocks, dtype=jnp.int32)[None, :]).astype(f32)
    col_hot = (tile_col[:, None] == jnp.arange(col_blocks, dtype=jnp.int32)[None, :]).astype(f32)
    live = (jnp.arange(slot_count, dtype=jnp.int32) < tile_count[0]).astype(f32)
    place = row_hot[:, :, None] * col_hot[:, None, :] * live[:, None, None]
    vec_hot = (tile_vector[:, None] == jnp.arange(vec_dev, dtype=jnp.int32)[None, :]).astype(f32)
    trial_blocks = trial_state.reshape(row_blocks, tile_size * electrons)
    tile_rows = jnp.dot(row_hot.astype(bf16), trial_blocks, preferred_element_type=f32).astype(bf16)
    tile_rows = tile_rows.reshape(slot_count, tile_size, electrons)
    projected = jnp.einsum(
        "tpq,tpn->tqn", chol_tiles, tile_rows, preferred_element_type=f32
    ).astype(bf16)
    theta_blocks = theta_new.reshape(walk_all, col_blocks, tile_size, electrons)
    scores = jnp.einsum("tqn,wcqn->wtc", projected, theta_blocks, preferred_element_type=f32)
    scores = jnp.sum(scores * col_hot[None], axis=2) * live[None, :]
    bias_part = jnp.dot(scores, vec_hot, precision=highest)
    force_bias = lax.psum(bias_part, "chol")
    field = (aux_noise - SQRT_TAU * force_bias).astype(bf16)
    coeff = jnp.dot(field, vec_hot.T.astype(bf16), preferred_element_type=f32)
    weights = (coeff[:, :, None, None] * place[None]).astype(bf16)
    spread = jnp.einsum("wtak,tpq->wapkq", weights, chol_tiles, preferred_element_type=f32)
    own_op = (
        lax.psum_scatter(
            spread.reshape(walk_dev * lax.axis_size("wide"), orbitals, orb_rows).astype(
                jnp.bfloat16
            ),
            "wide",
            scatter_dimension=0,
            tiled=True,
        )
        .astype(jnp.float32)
        .astype(bf16)
    )
    term = own_walkers
    total = own_walkers.astype(f32)
    for order in range(1, TAYLOR + 1):

        def product(start, count, current=term):
            return jnp.einsum("wpm,wmn->pwn", own_op, current, preferred_element_type=f32)

        summed = lax.psum_scatter(
            product(jnp.int32(0), orb_rows * lax.axis_size("chol")).astype(jnp.bfloat16),
            "chol",
            scatter_dimension=0,
            tiled=True,
        ).astype(jnp.float32)
        term = (SQRT_TAU / order * jnp.transpose(summed, (1, 0, 2))).astype(bf16)
        total = total + term.astype(f32)
    return (force_bias, total.astype(bf16))


def solution(mesh):
    return jax.shard_map(
        body,
        mesh=mesh,
        in_specs=(
            P("wide", "chol", None),
            P("wide", None, None),
            P(),
            P(("wide", "chol"), None, None),
            P(("wide", "chol")),
            P(("wide", "chol")),
            P(("wide", "chol")),
            P(("wide", "chol")),
            P(),
            P(None, "wide"),
        ),
        out_specs=(P(None, "wide"), P("wide", "chol", None)),
        check_vma=False,
    )
```

profile of v0, /device:TPU:0, one launch (start us, length us, event | category | flops | bytes accessed | tf_op | source)
XLA Modules:
  0.0 535.3 jit_solution(14423003403769741548)
XLA Ops:
  7.2 0.0 copy-start
  7.2 0.0 copy-start.9
  7.2 0.0 all-gather.6.cloned.1.call-start
  7.2 2.0 convolution_convert_fusion.5
  9.3 0.0 all-gather.6.cloned.1.call-update
  9.3 0.0 all-gather.4.cloned.1.call-start
  9.4 0.7 all-gather.4.cloned.1.call-update
  10.1 0.0 reduce-scatter.6.cloned.1.call-start
  10.1 1.6 reshape.172
  11.7 0.0 copy-done.9
  11.7 1.3 convolution_convert_fusion
  13.0 1.1 copy.33
  14.1 0.0 copy-done
  14.1 3.3 convert_bitcast_fusion.1
  17.4 0.0 copy-start.11
  17.4 0.0 copy-start.10
  17.4 6.8 %copy.21 = bf16[64,128,256]{2,0,1:T(8,128)(2,1)} copy(bf16[64,128,256]{1,2,0:T(8,128)(2,1)} %convert_bitcast_fusion.1) | data formatting | bytes 8388608 | tf_op jit(solution)/shard_map/convert_element_type | solution.py:58
  24.9 0.0 copy-done.11
  24.9 37.8 %all-gather.6.cloned.1.call-done = bf16[4096,256]{1,0:T(8,128)(2,1)} async-done(((bf16[512,256]{1,0:T(8,128)(2,1)}), bf16[4096,256]{1,0:T(8,128)(2,1)}) %all-gather.6.cloned.1.call-update) | async-done | bytes 2097168 | tf_op jit(solution)/shard_map/all_gather | solution.py:38
  62.7 0.0 copy-done.10
  62.7 3.1 fusion.15
  65.8 0.0 copy-done.3
  65.8 0.0 copy-start.12
  65.8 0.0 copy-start.8
  65.9 1.2 fusion.24
  67.1 0.0 copy-done.12
  67.1 0.2 fusion.42
  67.3 5.6 %psum.7 = f32[8,64]{1,0:T(8,128)S(1)} all-reduce(f32[8,64]{1,0:T(8,128)S(1)} %fusion.42), channel_id=1, replica_groups=mesh['wide'=8,'chol'=4] {'chol'}, use_global_device_ids=true, to_apply=%region_1.0 | all-reduce | flops 512 | bytes 4096 | tf_op jit(solution)/shard_map/psum | solution.py:63
  72.9 0.0 copy-done.8
  72.9 0.1 fusion.43
  73.0 9.3 %convert_bitcast_fusion = bf16[8,16,128,4,128]{4,1,2,3,0:T(8,128)(2,1)} fusion(bf16[64,128,128,1,1]{2,1,0,4,3:T(8,128)(2,1)S(1)} %bitcast.110, f32[64,16,4]{0,1,2:T(8,128)S(1)} %multiply_multiply_fusion, f32[8,64]{1,0:T(8,128)S(1)} %fusion.43), kind=kOutput, calls=%fused_computation.1 | convolution fusion | flops 1082195968 | bytes 18892800 | tf_op jit(solution)/shard_map/wtak,tpq->wapkq/dot_general | solution.py:67
  82.3 0.0 copy-done.7
  82.3 25.5 %copy.23 = bf16[8,16,128,4,128]{2,1,4,3,0:T(8,128)(2,1)} copy(bf16[8,16,128,4,128]{4,1,2,3,0:T(8,128)(2,1)} %convert_bitcast_fusion) | data formatting | bytes 33554432 | tf_op jit(solution)/shard_map/convert_element_type | solution.py:70
  107.8 25.3 %convert_element_type.212 = bf16[8,2048,512]{1,2,0:T(8,128)(2,1)} reshape(bf16[8,16,128,4,128]{2,1,4,3,0:T(8,128)(2,1)} %copy.23) | data formatting | bytes 33554432 | tf_op jit(solution)/shard_map/convert_element_type | solution.py:70
  133.1 0.0 reduce-scatter.6.cloned.1.call-update
  133.1 0.2 reduce-scatter.8.cloned.1.call-start
  133.4 0.1 iota_compare_fusion.4
  133.5 3.0 fusion.11
  136.5 0.7 copy.28
  137.1 277.7 %reduce-scatter.6.cloned.1.call-done = bf16[1,2048,512]{1,2,0:T(8,128)(2,1)} async-done(((bf16[8,2048,512]{1,2,0:T(8,128)(2,1)}), bf16[1,2048,512]{1,2,0:T(8,128)(2,1)}) %reduce-scatter.6.cloned.1.call-update) | async-done | bytes 2097168 | tf_op jit(solution)/shard_map/reduce_scatter | solution.py:69
  414.9 3.4 fusion.2
  418.3 0.0 reduce-scatter.8.cloned.1.call-update
  418.3 0.0 reduce-scatter.10.cloned.1.call-start
  418.4 24.0 %reduce-scatter.8.cloned.1.call-done = bf16[512,1,256]{0,2,1:T(8,128)(2,1)} async-done(((bf16[2048,1,256]{0,2,1:T(8,128)(2,1)}), bf16[512,1,256]{0,2,1:T(8,128)(2,1)}) %reduce-scatter.8.cloned.1.call-update) | async-done | bytes 262160 | tf_op jit(solution)/shard_map/reduce_scatter | solution.py:87
  442.4 0.0 copy-done.2
  442.4 2.6 fusion.3
  445.0 0.0 reduce-scatter.10.cloned.1.call-update
  445.1 0.0 reduce-scatter.12.cloned.1.call-start
  445.1 25.0 %reduce-scatter.10.cloned.1.call-done = bf16[512,1,256]{0,2,1:T(8,128)(2,1)} async-done(((bf16[2048,1,256]{0,2,1:T(8,128)(2,1)}), bf16[512,1,256]{0,2,1:T(8,128)(2,1)}) %reduce-scatter.10.cloned.1.call-update) | async-done | bytes 262160 | tf_op jit(solution)/shard_map/reduce_scatter | solution.py:87
  470.1 2.6 fusion.4
  472.8 0.0 reduce-scatter.12.cloned.1.call-update
  472.8 0.0 copy-start.4
  472.8 0.0 copy-start.5
  472.8 0.0 reduce-scatter.14.cloned.1.call-start
  472.8 25.0 %reduce-scatter.12.cloned.1.call-done = bf16[512,1,256]{0,2,1:T(8,128)(2,1)} async-done(((bf16[2048,1,256]{0,2,1:T(8,128)(2,1)}), bf16[512,1,256]{0,2,1:T(8,128)(2,1)}) %reduce-scatter.12.cloned.1.call-update) | async-done | bytes 262160 | tf_op jit(solution)/shard_map/reduce_scatter | solution.py:87
  497.8 3.5 fusion.5
  501.3 0.0 reduce-scatter.14.cloned.1.call-update
  501.3 25.0 %reduce-scatter.14.cloned.1.call-done = bf16[512,1,256]{0,2,1:T(8,128)(2,1)} async-done(((bf16[2048,1,256]{0,2,1:T(8,128)(2,1)}), bf16[512,1,256]{0,2,1:T(8,128)(2,1)}) %reduce-scatter.14.cloned.1.call-update) | async-done | bytes 262160 | tf_op jit(solution)/shard_map/reduce_scatter | solution.py:87
  526.4 0.0 copy-done.4
  526.4 0.0 copy-done.5
  526.4 0.0 copy-done.6
  526.4 1.2 fusion.32
  527.6 0.8 copy.24
  528.4 0.0 copy-done.1
  (10 shorter events, 0.0 us)
Async XLA Ops:
  7.2 6.9 %copy-start = (bf16[64,128,128]{2,1,0:T(8,128)(2,1)S(1)}, bf16[64,128,128]{2,1,0:T(8,128)(2,1)}, u32[]{:S(2)}) copy-start(bf16[64,128,128]{2,1,0:T(8,128)(2,1)} %param.13) | copy-start | bytes 6291460
  7.2 4.5 copy-start.9
  7.2 55.5 %all-gather.6.cloned.1.call-start = ((), (), s32[]{:S(2)}) async-start(), calls=%async_computation.11 | async-start | bytes 2359296 | tf_op jit(solution)/shard_map/all_gather | solution.py:38
  9.3 124.1 %all-gather.4.cloned.1.call-start = ((), (), s32[]{:S(2)}) async-start(), calls=%async_computation.5 | async-start | bytes 2359296 | tf_op jit(solution)/shard_map/all_gather | solution.py:37
  10.1 404.8 %reduce-scatter.6.cloned.1.call-start = ((), (), s32[]{:S(2)}) async-start(), calls=%async_computation.6 | async-start | bytes 18874368 | tf_op jit(solution)/shard_map/reduce_scatter | solution.py:69
  17.4 7.5 %copy-start.11 = (s32[64]{0:T(128)S(1)}, s32[64]{0:T(128)}, u32[]{:S(2)}) copy-start(s32[64]{0:T(128)} %param.16) | copy-start | bytes 772
  17.4 45.4 %copy-start.10 = (s32[8]{0:T(128)S(1)}, s32[8]{0:T(128)}, u32[]{:S(2)}) copy-start(s32[8]{0:T(128)} %param.18) | copy-start | bytes 100
  62.7 3.1 copy-start.3
  65.8 1.2 copy-start.12
  65.8 7.1 %copy-start.8 = (f32[8,64]{1,0:T(8,128)S(1)}, f32[8,64]{1,0:T(8,128)}, u32[]{:S(2)}) copy-start(f32[8,64]{1,0:T(8,128)} %param.19) | copy-start | bytes 6148
  72.9 9.4 %copy-start.7 = (f32[8,64]{1,0:T(8,128)}, f32[8,64]{1,0:T(8,128)S(1)}, u32[]{:S(2)}) copy-start(f32[8,64]{1,0:T(8,128)S(1)} %psum.7) | copy-start | bytes 6148
  133.1 309.3 %reduce-scatter.8.cloned.1.call-start = ((), (), s32[]{:S(2)}) async-start(), calls=%async_computation.7 | async-start | bytes 1310720 | tf_op jit(solution)/shard_map/reduce_scatter | solution.py:87
  414.9 27.5 %copy-start.2 = (bf16[1,2048,512]{1,2,0:T(8,128)(2,1)S(1)}, bf16[1,2048,512]{1,2,0:T(8,128)(2,1)}, u32[]{:S(2)}) copy-start(bf16[1,2048,512]{1,2,0:T(8,128)(2,1)} %reduce-scatter.6.cloned.1.call-done) | copy-start | bytes 6291460
  418.3 51.8 %reduce-scatter.10.cloned.1.call-start = ((), (), s32[]{:S(2)}) async-start(), calls=%async_computation.8 | async-start | bytes 1310720 | tf_op jit(solution)/shard_map/reduce_scatter | solution.py:87
  445.1 52.7 %reduce-scatter.12.cloned.1.call-start = ((), (), s32[]{:S(2)}) async-start(), calls=%async_computation.9 | async-start | bytes 1310720 | tf_op jit(solution)/shard_map/reduce_scatter | solution.py:87
  472.8 53.6 %copy-start.4 = (bf16[512,1,256]{0,2,1:T(8,128)(2,1)S(1)}, bf16[512,1,256]{0,2,1:T(8,128)(2,1)}, u32[]{:S(2)}) copy-start(bf16[512,1,256]{0,2,1:T(8,128)(2,1)} %reduce-scatter.8.cloned.1.call-done) | copy-start | bytes 786436
  472.8 53.6 %copy-start.5 = (bf16[512,1,256]{0,2,1:T(8,128)(2,1)S(1)}, bf16[512,1,256]{0,2,1:T(8,128)(2,1)}, u32[]{:S(2)}) copy-start(bf16[512,1,256]{0,2,1:T(8,128)(2,1)} %reduce-scatter.10.cloned.1.call-done) | copy-start | bytes 786436
  472.8 53.6 %reduce-scatter.14.cloned.1.call-start = ((), (), s32[]{:S(2)}) async-start(), calls=%async_computation.10 | async-start | bytes 1310720 | tf_op jit(solution)/shard_map/reduce_scatter | solution.py:87
  497.8 28.6 %copy-start.6 = (bf16[512,1,256]{0,2,1:T(8,128)(2,1)S(1)}, bf16[512,1,256]{0,2,1:T(8,128)(2,1)}, u32[]{:S(2)}) copy-start(bf16[512,1,256]{0,2,1:T(8,128)(2,1)} %reduce-scatter.12.cloned.1.call-done) | copy-start | bytes 786436
  497.8 30.6 %copy-start.1 = (bf16[64,128,128]{2,1,0:T(8,128)(2,1)S(1)}, bf16[64,128,128]{2,1,0:T(8,128)(2,1)}, u32[]{:S(2)}) copy-start(bf16[64,128,128]{2,1,0:T(8,128)(2,1)} %param.13) | copy-start | bytes 6291460
Sparse Core Ops, SparseCore 0:
  10.7 51.9 all-gather.5
  64.9 47.7 all-gather.3
  133.3 281.5 reduce-scatter.5
  418.4 23.9 reduce-scatter.7
  445.2 24.8 reduce-scatter.9
  472.9 24.8 reduce-scatter.11
  501.5 24.8 reduce-scatter.13
where the time goes:
time: 537 us; the launch traced here: 535 us
  waiting for transfers between devices  415 us (77%)
  local copies, waits for them, and re-layouts  61.9 us (12%)
  matrix products  35.7 us (7%)
  between operations  15 us (3%)
  blocking collectives  5.65 us (1%)
    reduce_scatter x1, waiting for transfers between devices, body(): lax.psum_scatter(spread.reshape(walk_dev * lax.axis_size('wide'), orbital...  278 us
    reduce_scatter x4, waiting for transfers between devices, body(): lax.psum_scatter(product(jnp.int32(0), orb_rows * lax.axis_size('chol'))....  99 us
    convert_element_type x2, local copies, waits for them, and re-layouts, body(): spread.reshape(walk_dev * lax.axis_size('wide'), orbitals, orb_rows)  50.8 us
    all_gather x1, waiting for transfers between devices, body(): lax.all_gather(theta_own, 'wide', axis=0, tiled=True)  37.8 us
    dot_general x4, matrix products, product(): jnp.einsum('wpm,wmn->pwn', own_op, current, preferred_element_type=f32)  12.2 us
  transfers between devices with their start and end apart: 7, of which 6 were waited for; matrix products, arithmetic and copies ran while one was open for 15% of the time, Pallas kernels for 0%

commit v1 on v0

v1 whole, which is shorter than its diff:
```python
import jax
import jax.numpy as jnp
from jax import lax
from jax.sharding import PartitionSpec as P

TAYLOR = 4


SQRT_TAU = 0.1


def ring_order(size):
    half = size // 2
    return [2 * p for p in range(half)] + [2 * (size - 1 - p) + 1 for p in range(half, size)]


def body(
    walkers,
    intersection_inv,
    trial_state,
    chol_tiles,
    tile_vector,
    tile_row,
    tile_col,
    tile_count,
    sources,
    aux_noise,
):
    f32 = jnp.float32
    bf16 = jnp.bfloat16
    highest = lax.Precision.HIGHEST
    walk_dev, orb_rows, electrons = walkers.shape
    slot_count, tile_size, _ = chol_tiles.shape
    orbitals = trial_state.shape[0]
    row_blocks = orbitals // tile_size
    col_blocks = orb_rows // tile_size
    walk_all, vec_dev = aux_noise.shape
    wide = lax.axis_size("wide")
    me = lax.axis_index("wide")
    live_slot = jnp.arange(slot_count, dtype=jnp.int32) < tile_count[0]
    place_own = jnp.where(live_slot, tile_row * col_blocks + tile_col, -1)
    meta = lax.all_gather(jnp.stack([place_own, tile_vector]), "wide", axis=0)
    walker_rows = lax.all_gather(walkers, "wide", axis=0, tiled=True)
    inv_all = lax.all_gather(intersection_inv, "wide", axis=0, tiled=True)
    order = ring_order(wide)
    right = [(order[p], order[(p + 1) % wide]) for p in range(wide)]
    left = [(b, a) for a, b in right]
    spot_of = [0] * wide
    for p, idx in enumerate(order):
        spot_of[idx] = p
    turns = [0] + [turn for step in range(1, wide) for turn in (-step, step)]
    owners = jnp.asarray(
        [[order[(spot_of[idx] + turn) % wide] for turn in turns] for idx in range(wide)], jnp.int32
    )[me]
    half = slot_count // 2
    going, coming = chol_tiles[:half], chol_tiles[half:]
    parts = [chol_tiles]
    for step in range(1, wide):
        going = lax.ppermute(going, "wide", right)
        coming = lax.ppermute(coming, "wide", left)
        parts += [going, coming]
    picker = (sources[:, None] == jnp.arange(walk_all, dtype=jnp.int32)[None, :]).astype(bf16)
    picked = jnp.einsum("jw,wmn->jmn", picker, walker_rows, preferred_element_type=f32).astype(bf16)
    picked_inv = jnp.einsum("jw,wnk->jnk", picker, inv_all, preferred_element_type=f32).astype(bf16)
    theta_new = jnp.einsum("jmn,jnk->jmk", picked, picked_inv, preferred_element_type=f32).astype(
        bf16
    )
    own_walkers = lax.dynamic_slice_in_dim(picked, me * walk_dev, walk_dev, 0)
    row_hot = (tile_row[:, None] == jnp.arange(row_blocks, dtype=jnp.int32)[None, :]).astype(f32)
    col_hot = (tile_col[:, None] == jnp.arange(col_blocks, dtype=jnp.int32)[None, :]).astype(f32)
    live = live_slot.astype(f32)
    vec_hot = (tile_vector[:, None] == jnp.arange(vec_dev, dtype=jnp.int32)[None, :]).astype(f32)
    trial_blocks = trial_state.reshape(row_blocks, tile_size * electrons)
    tile_rows = jnp.dot(row_hot.astype(bf16), trial_blocks, preferred_element_type=f32).astype(bf16)
    tile_rows = tile_rows.reshape(slot_count, tile_size, electrons)
    projected = jnp.einsum(
        "tpq,tpn->tqn", chol_tiles, tile_rows, preferred_element_type=f32
    ).astype(bf16)
    theta_blocks = theta_new.reshape(walk_all, col_blocks, tile_size, electrons)
    scores = jnp.einsum("tqn,wcqn->wtc", projected, theta_blocks, preferred_element_type=f32)
    scores = jnp.sum(scores * col_hot[None], axis=2) * live[None, :]
    bias_part = jnp.dot(scores, vec_hot, precision=highest)
    force_bias = lax.psum(bias_part, "chol")
    field = (aux_noise - SQRT_TAU * force_bias).astype(bf16)
    field_all = lax.all_gather(field, "wide", axis=0)
    own_field = lax.dynamic_index_in_dim(field_all, me * walk_dev, 1, keepdims=False)
    places = row_blocks * col_blocks
    place_all, vec_all = meta[:, 0], meta[:, 1]
    vec_hot_all = (vec_all[:, :, None] == jnp.arange(vec_dev, dtype=jnp.int32)).astype(f32)
    coeff = jnp.sum(vec_hot_all * own_field.astype(f32)[:, None, :], axis=2)

    def in_parts(whole):
        picked_rows = jnp.sum(
            jnp.where(
                owners[:, None, None] == jnp.arange(wide, dtype=jnp.int32)[None, :, None],
                whole[None],
                jnp.zeros((), whole.dtype),
            ),
            axis=1,
        )
        ends = jnp.stack([picked_rows[1::2, :half], picked_rows[2::2, half:]], axis=1)
        return jnp.concatenate([picked_rows[0], ends.reshape(-1)])

    weights_in = jnp.where(
        in_parts(place_all)[None, :] == jnp.arange(places, dtype=jnp.int32)[:, None],
        in_parts(coeff)[None, :],
        0.0,
    ).astype(bf16)
    tiles_in = jnp.concatenate(parts, axis=0)
    spread = jnp.einsum(
        "akt,tpq->apkq",
        weights_in.reshape(row_blocks, col_blocks, -1),
        tiles_in,
        preferred_element_type=f32,
    ).astype(bf16)
    own_op = spread.reshape(1, orbitals, orb_rows)
    term = own_walkers
    total = own_walkers.astype(f32)
    for order in range(1, TAYLOR + 1):
        product = jnp.einsum("wpm,wmn->pwn", own_op, term, preferred_element_type=f32)
        summed = lax.psum_scatter(
            product.astype(bf16), "chol", scatter_dimension=0, tiled=True
        ).astype(f32)
        term = (SQRT_TAU / order * jnp.transpose(summed, (1, 0, 2))).astype(bf16)
        total = total + term.astype(f32)
    return (force_bias, total.astype(bf16))


def solution(mesh):
    return jax.shard_map(
        body,
        mesh=mesh,
        in_specs=(
            P("wide", "chol", None),
            P("wide", None, None),
            P(),
            P(("wide", "chol"), None, None),
            P(("wide", "chol")),
            P(("wide", "chol")),
            P(("wide", "chol")),
            P(("wide", "chol")),
            P(),
            P(None, "wide"),
        ),
        out_specs=(P(None, "wide"), P("wide", "chol", None)),
        check_vma=False,
    )
```

time: 537 us -> 496 us (0.924)
  waiting for transfers between devices: 415 us -> 269 us
  blocking collectives: 5.65 us -> 82.3 us
  starting transfers between devices: 0.47 us -> 23.3 us
  other arithmetic: 1.28 us -> 10.6 us
    reduce_scatter x5 -> x0, waiting for transfers between devices: 377 us -> none  [the longest x1 278 us: body(): lax.psum_scatter(spread.reshape(walk_dev * lax.axis_size('wide'), orbital...]
    unnamed x7 -> x10, waiting for transfers between devices: 0.79 us -> 205 us
    all_gather x0 -> x2, blocking collectives: none -> 76.3 us  [the longest x1 44.5 us: body(): meta = lax.all_gather(jnp.stack([place_own, tile_vector]), 'wide', axis=0)]
    ppermute x0 -> x14, waiting for transfers between devices: none -> 63.8 us  [the longest x7 58.5 us: body(): going = lax.ppermute(going, 'wide', right)]
    convert_element_type x3 -> x5, local copies, waits for them, and re-layouts: 57.6 us -> 19 us  [the longest x4 15.2 us: body(): product.astype(bf16)]
    all_gather x2, waiting for transfers between devices: 37.8 us -> 0.01 us  [the longest x1 0.01 us: body(): inv_all = lax.all_gather(intersection_inv, 'wide', axis=0, tiled=True)]
    unnamed x28 -> x41, local copies, waits for them, and re-layouts: 2.01 us -> 33.2 us
    ppermute x0 -> x14, starting transfers between devices: none -> 22.8 us  [the longest x7 13.1 us: body(): going = lax.ppermute(going, 'wide', right)]
  transfers between devices with their start and end apart: 7 -> 20, of which waited for: 6 -> 9; matrix products, arithmetic and copies ran while one was open for 15% -> 12% of each run, Pallas kernels for 0% -> 0%
where the time goes in v1:
time: 496 us; the launch traced here: 495 us
  waiting for transfers between devices  269 us (54%)
  blocking collectives  82.3 us (17%)
  local copies, waits for them, and re-layouts  62.5 us (13%)
  matrix products  31.9 us (6%)
  starting transfers between devices  23.3 us (5%)
  between operations  15.7 us (3%)
  other arithmetic  10.6 us (2%)
    unnamed x10, waiting for transfers between devices  205 us
    ppermute x7, waiting for transfers between devices, body(): going = lax.ppermute(going, 'wide', right)  58.5 us
    all_gather x1, blocking collectives, body(): meta = lax.all_gather(jnp.stack([place_own, tile_vector]), 'wide', axis=0)  44.5 us
    unnamed x41, local copies, waits for them, and re-layouts  33.2 us
    all_gather x1, blocking collectives, body(): field_all = lax.all_gather(field, 'wide', axis=0)  31.8 us
    convert_element_type x4, local copies, waits for them, and re-layouts, body(): product.astype(bf16)  15.2 us
    ppermute x7, starting transfers between devices, body(): going = lax.ppermute(going, 'wide', right)  13.1 us
  transfers between devices with their start and end apart: 20, of which 9 were waited for; matrix products, arithmetic and copies ran while one was open for 12% of the time, Pallas kernels for 0%

profile of v1, /device:TPU:0, one launch (start us, length us, event | category | flops | bytes accessed | tf_op | source)
XLA Modules:
  0.0 495.1 jit_solution(13164088525227858607)
XLA Ops:
  8.0 1.8 fusion.77
  9.8 1.7 copy.136
  11.5 3.0 collective-permute-start
  16.0 44.5 %all-gather.2 = s32[8,2,64]{2,1,0:T(2,128)S(1)} all-gather(s32[1,2,64]{2,1,0:T(2,128)S(1)} %add_bitcast_fusion), channel_id=2, replica_groups=mesh['wide'=8,'chol'=4] {'wide'}, dimensions={0}, use_global_device_ids=true | all-gather | bytes 4608 | tf_op jit(solution)/shard_map/all_gather | solution.py:42
  60.6 0.7 fusion.74
  61.3 2.4 collective-permute-start.3
  64.7 1.3 convolution_convert_fusion
  66.0 30.7 %collective-permute-done.2 = bf16[32,128,128]{2,0,1:T(8,128)(2,1)} collective-permute-done((bf16[32,128,128]{2,0,1:T(8,128)(2,1)S(1)}, bf16[32,128,128]{2,0,1:T(8,128)(2,1)}, u32[]{:S(2)}, u32[]{:S(2)}) %collective-permute-start.2) | collective-permute-done | bytes 1048608 | tf_op jit(solution)/shard_map/ppermute | solution.py:59
  96.6 2.6 collective-permute-start.4
  99.2 5.3 %collective-permute-done.3 = bf16[32,128,128]{2,0,1:T(8,128)(2,1)} collective-permute-done((bf16[32,128,128]{2,0,1:T(8,128)(2,1)}, bf16[32,128,128]{2,0,1:T(8,128)(2,1)}, u32[]{:S(2)}, u32[]{:S(2)}) %collective-permute-start.3) | collective-permute-done | bytes 1048608 | tf_op jit(solution)/shard_map/ppermute | solution.py:60
  104.5 3.6 collective-permute-start.5
  108.1 1.1 copy.79
  109.7 2.7 constant_dynamic-update-slice_fusion.14
  112.4 3.3 convert_bitcast_fusion
  115.6 15.8 %collective-permute-done.4 = bf16[32,128,128]{2,0,1:T(8,128)(2,1)S(1)} collective-permute-done((bf16[32,128,128]{2,0,1:T(8,128)(2,1)}, bf16[32,128,128]{2,0,1:T(8,128)(2,1)S(1)}, u32[]{:S(2)}, u32[]{:S(2)}) %collective-permute-start.4) | collective-permute-done | bytes 1048608 | tf_op jit(solution)/shard_map/ppermute | solution.py:59
  131.5 2.4 collective-permute-start.6
  133.8 0.7 collective-permute-start.7
  134.6 1.2 constant_dynamic-update-slice_fusion.13
  135.7 2.4 constant_dynamic-update-slice_fusion.12
  138.1 1.9 convolution_convert_fusion.5
  140.1 2.4 constant_dynamic-update-slice_fusion.11
  142.5 2.4 constant_dynamic-update-slice_fusion.10
  144.9 1.2 constant_dynamic-update-slice_fusion.9
  146.1 1.2 constant_dynamic-update-slice_fusion.8
  147.2 7.1 %collective-permute-done.6 = bf16[32,128,128]{2,0,1:T(8,128)(2,1)} collective-permute-done((bf16[32,128,128]{2,0,1:T(8,128)(2,1)S(1)}, bf16[32,128,128]{2,0,1:T(8,128)(2,1)}, u32[]{:S(2)}, u32[]{:S(2)}) %collective-permute-start.6) | collective-permute-done | bytes 1048608 | tf_op jit(solution)/shard_map/ppermute | solution.py:59
  154.4 2.6 collective-permute-start.8
  157.0 0.7 collective-permute-start.9
  157.7 2.9 fusion.17
  160.6 2.1 fusion.20
  162.7 4.3 copy.59
  167.1 6.4 %fusion.35 = f32[8,64]{1,0:T(8,128)S(1)} fusion(bf16[8,4,128,256]{2,0,3,1:T(8,128)(2,1)} %copy.59, bf16[64,128,256]{1,2,0:T(8,128)(2,1)} %convert_bitcast_fusion, f32[64,4]{0,1:T(4,128)S(1)} %fusion.73), kind=kOutput, calls=%fused_computation.33 | convolution fusion | flops 134221312 | bytes 6294528 | tf_op jit(solution)/shard_map/tqn,wcqn->wtc/dot_general | solution.py:80
  173.5 4.8 collective-permute-done.8
  178.4 2.3 collective-permute-start.10
  181.2 6.0 %psum.7 = f32[8,64]{1,0:T(8,128)S(1)} all-reduce(f32[8,64]{1,0:T(8,128)S(1)} %fusion.63), channel_id=1, replica_groups=mesh['wide'=8,'chol'=4] {'chol'}, use_global_device_ids=true, to_apply=%region_1.2 | all-reduce | flops 512 | bytes 4096 | tf_op jit(solution)/shard_map/psum | solution.py:83
  187.3 31.8 %all-gather.1 = bf16[64,64]{1,0:T(8,128)(2,1)S(1)} all-gather(bf16[8,64]{1,0:T(8,128)(2,1)S(1)} %subtract_convert_fusion), channel_id=3, replica_groups=mesh['wide'=8,'chol'=4] {'wide'}, dimensions={0}, use_global_device_ids=true | all-gather | bytes 9216 | tf_op jit(solution)/shard_map/all_gather | solution.py:85
  219.9 1.4 constant_dynamic-slice_fusion.1
  221.2 1.9 collective-permute-start.13
  223.2 2.4 constant_dynamic-update-slice_fusion.7
  225.6 2.4 constant_dynamic-update-slice_fusion.6
  228.0 2.4 constant_dynamic-update-slice_fusion.5
  230.4 2.4 constant_dynamic-update-slice_fusion.4
  232.9 1.2 constant_dynamic-update-slice_fusion.3
  234.1 2.4 constant_dynamic-update-slice_fusion.2
  236.5 1.2 constant_dynamic-update-slice_fusion.1
  237.8 1.2 constant_dynamic-update-slice_fusion
  238.9 8.9 %convert_bitcast_fusion.1 = bf16[16,128,4,128]{3,0,2,1:T(8,128)(2,1)S(1)} fusion(bf16[512,128,128]{2,0,1:T(8,128)(2,1)} %constant_dynamic-update-slice_fusion, bf16[512]{0:T(512)(128)(2,1)S(1)} %pad_maximum_fusion.1, s32[16,4]{0,1:T(4,128)S(1)} %multiply_add_fusion, s32[512]{0:T(512)S(1)} %pad_add_fusion.1), kind=kOutput, calls=%fused_computation.23 | convolution fusion | flops 1074855936 | bytes 18877696 | tf_op jit(solution)/shard_map/akt,tpq->apkq/dot_general | solution.py:110
  247.8 3.8 copy.66
  251.7 2.6 fusion.5
  254.3 3.8 copy.67
  259.4 49.6 %all-reduce.9.cloned.1.call-done = bf16[2048,1,256]{2,1,0:T(2,128)(2,1)} async-done(((bf16[2048,1,256]{2,1,0:T(2,128)(2,1)}), bf16[2048,1,256]{2,1,0:T(2,128)(2,1)}) %all-reduce.9.cloned.1.call-update) | async-done | bytes 1048592
  309.1 1.8 fusion.48
  310.8 0.7 fusion.6
  311.6 3.8 copy.68
  315.5 51.6 %all-reduce.11.cloned.1.call-done = bf16[2048,1,256]{2,1,0:T(2,128)(2,1)} async-done(((bf16[2048,1,256]{2,1,0:T(2,128)(2,1)}), bf16[2048,1,256]{2,1,0:T(2,128)(2,1)}) %all-reduce.11.cloned.1.call-update) | async-done | bytes 1048592
  367.0 1.8 fusion.46
  368.8 0.7 fusion.7
  369.5 3.8 copy.69
  373.7 51.3 %all-reduce.13.cloned.1.call-done = bf16[2048,1,256]{2,1,0:T(2,128)(2,1)} async-done(((bf16[2048,1,256]{2,1,0:T(2,128)(2,1)}), bf16[2048,1,256]{2,1,0:T(2,128)(2,1)}) %all-reduce.13.cloned.1.call-update) | async-done | bytes 1048592
  425.0 1.8 fusion.44
  426.7 0.7 fusion.8
  427.5 3.8 copy.70
  431.3 51.6 %all-reduce.15.cloned.1.call-done = bf16[2048,1,256]{2,1,0:T(2,128)(2,1)} async-done(((bf16[2048,1,256]{2,1,0:T(2,128)(2,1)}), bf16[2048,1,256]{2,1,0:T(2,128)(2,1)}) %all-reduce.15.cloned.1.call-update) | async-done | bytes 1048592
  482.9 4.6 fusion.40
  487.5 0.7 copy.71
  (79 shorter events, 5.5 us)
Async XLA Ops:
  7.2 131.0 %all-gather.8.cloned.1.call-start = ((), (), s32[]{:S(2)}) async-start(), calls=%async_computation.1 | async-start | bytes 1179648 | tf_op jit(solution)/shard_map/all_gather | solution.py:44
  7.9 8.1 %copy-start.7 = (s32[64]{0:T(128)S(1)}, s32[64]{0:T(128)}, u32[]{:S(2)}) copy-start(s32[64]{0:T(128)} %param.17) | copy-start | bytes 772
  7.9 8.1 %copy-start.8 = (s32[64]{0:T(128)S(1)}, s32[64]{0:T(128)}, u32[]{:S(2)}) copy-start(s32[64]{0:T(128)} %param.16) | copy-start | bytes 772
  7.9 8.1 %copy-start.9 = (s32[64]{0:T(128)S(1)}, s32[64]{0:T(128)}, u32[]{:S(2)}) copy-start(s32[64]{0:T(128)} %param.15) | copy-start | bytes 772
  7.9 56.0 %copy-start.3 = (bf16[2048,256]{1,0:T(8,128)(2,1)S(1)}, bf16[2048,256]{1,0:T(8,128)(2,1)}, u32[]{:S(2)}) copy-start(bf16[2048,256]{1,0:T(8,128)(2,1)} %param.13) | copy-start | bytes 3145732
  7.9 149.8 %all-gather.6.cloned.1.call-start = ((), (), s32[]{:S(2)}) async-start(), calls=%async_computation | async-start | bytes 2359296 | tf_op jit(solution)/shard_map/all_gather | solution.py:43
  11.5 49.8 %collective-permute-start = (bf16[32,128,128]{2,0,1:T(8,128)(2,1)}, bf16[32,128,128]{2,0,1:T(8,128)(2,1)S(1)}, u32[]{:S(2)}, u32[]{:S(2)}) collective-permute-start(bf16[32,128,128]{2,0,1:T(8,128)(2,1)} %copy.136), channel_id=1, source_target_pairs={{0,8},{8,16},{16,24},{24,28},{28,20},{20,12},{12,4},{4,0},{1,9},{9... | collective-permute-start | bytes 3145736 | tf_op jit(solution)/shard_map/ppermute | solution.py:59
  15.2 46.1 %collective-permute-start.1 = (bf16[32,128,128]{2,0,1:T(8,128)(2,1)S(1)}, bf16[32,128,128]{2,0,1:T(8,128)(2,1)}, u32[]{:S(2)}, u32[]{:S(2)}) collective-permute-start(bf16[32,128,128]{2,0,1:T(8,128)(2,1)S(1)} %copy.137), channel_id=1, source_target_pairs={{8,0},{16,8},{24,16},{28,24},{20,28},{12,20},{4,12},{0,4},{9,1},{1... | collective-permute-start | bytes 3145736 | tf_op jit(solution)/shard_map/ppermute | solution.py:60
  15.3 293.8 %all-reduce.9.cloned.1.call-start = ((), (), s32[]{:S(2)}) async-start(), calls=%async_computation.2 | async-start | bytes 4194304
  61.3 35.4 %collective-permute-start.2 = (bf16[32,128,128]{2,0,1:T(8,128)(2,1)S(1)}, bf16[32,128,128]{2,0,1:T(8,128)(2,1)}, u32[]{:S(2)}, u32[]{:S(2)}) collective-permute-start(bf16[32,128,128]{2,0,1:T(8,128)(2,1)S(1)} %collective-permute-done), channel_id=1, source_target_pairs={{0,8},{8,16},{16,24},{24,28},{28,20},{20,12},{12,4},{4,0},{1,9},{9... | collective-permute-start | bytes 3145736 | tf_op jit(solution)/shard_map/ppermute | solution.py:59
  61.3 43.3 %collective-permute-start.3 = (bf16[32,128,128]{2,0,1:T(8,128)(2,1)}, bf16[32,128,128]{2,0,1:T(8,128)(2,1)}, u32[]{:S(2)}, u32[]{:S(2)}) collective-permute-start(bf16[32,128,128]{2,0,1:T(8,128)(2,1)} %collective-permute-done.1), channel_id=1, source_target_pairs={{8,0},{16,8},{24,16},{28,24},{20,28},{12,20},{4,12},{0,4},{9,1},{1... | collective-permute-start | bytes 3145736 | tf_op jit(solution)/shard_map/ppermute | solution.py:60
  96.6 34.8 %collective-permute-start.4 = (bf16[32,128,128]{2,0,1:T(8,128)(2,1)}, bf16[32,128,128]{2,0,1:T(8,128)(2,1)S(1)}, u32[]{:S(2)}, u32[]{:S(2)}) collective-permute-start(bf16[32,128,128]{2,0,1:T(8,128)(2,1)} %collective-permute-done.2), channel_id=1, source_target_pairs={{0,8},{8,16},{16,24},{24,28},{28,20},{20,12},{12,4},{4,0},{1,9},{9... | collective-permute-start | bytes 3145736 | tf_op jit(solution)/shard_map/ppermute | solution.py:59
  104.5 29.3 %collective-permute-start.5 = (bf16[32,128,128]{2,0,1:T(8,128)(2,1)}, bf16[32,128,128]{2,0,1:T(8,128)(2,1)S(1)}, u32[]{:S(2)}, u32[]{:S(2)}) collective-permute-start(bf16[32,128,128]{2,0,1:T(8,128)(2,1)} %collective-permute-done.3), channel_id=1, source_target_pairs={{8,0},{16,8},{24,16},{28,24},{20,28},{12,20},{4,12},{0,4},{9,1},{1... | collective-permute-start | bytes 3145736 | tf_op jit(solution)/shard_map/ppermute | solution.py:60
  108.1 1.6 copy-start
  115.6 22.5 %copy-start.6 = (s32[8]{0:T(128)S(1)}, s32[8]{0:T(128)}, u32[]{:S(2)}) copy-start(s32[8]{0:T(128)} %param.19) | copy-start | bytes 100
  131.5 22.9 %collective-permute-start.6 = (bf16[32,128,128]{2,0,1:T(8,128)(2,1)S(1)}, bf16[32,128,128]{2,0,1:T(8,128)(2,1)}, u32[]{:S(2)}, u32[]{:S(2)}) collective-permute-start(bf16[32,128,128]{2,0,1:T(8,128)(2,1)S(1)} %collective-permute-done.4), channel_id=1, source_target_pairs={{0,8},{8,16},{16,24},{24,28},{28,20},{20,12},{12,4},{4,0},{1,9},{9... | collective-permute-start | bytes 3145736 | tf_op jit(solution)/shard_map/ppermute | solution.py:59
  133.8 23.1 %collective-permute-start.7 = (bf16[32,128,128]{2,0,1:T(8,128)(2,1)S(1)}, bf16[32,128,128]{2,0,1:T(8,128)(2,1)}, u32[]{:S(2)}, u32[]{:S(2)}) collective-permute-start(bf16[32,128,128]{2,0,1:T(8,128)(2,1)S(1)} %collective-permute-done.5), channel_id=1, source_target_pairs={{8,0},{16,8},{24,16},{28,24},{20,28},{12,20},{4,12},{0,4},{9,1},{1... | collective-permute-start | bytes 3145736 | tf_op jit(solution)/shard_map/ppermute | solution.py:60
  154.4 24.0 %collective-permute-start.8 = (bf16[32,128,128]{2,0,1:T(8,128)(2,1)}, bf16[32,128,128]{2,0,1:T(8,128)(2,1)}, u32[]{:S(2)}, u32[]{:S(2)}) collective-permute-start(bf16[32,128,128]{2,0,1:T(8,128)(2,1)} %collective-permute-done.6), channel_id=1, source_target_pairs={{0,8},{8,16},{16,24},{24,28},{28,20},{20,12},{12,4},{4,0},{1,9},{9... | collective-permute-start | bytes 3145736 | tf_op jit(solution)/shard_map/ppermute | solution.py:59
  157.0 23.7 %collective-permute-start.9 = (bf16[32,128,128]{2,0,1:T(8,128)(2,1)}, bf16[32,128,128]{2,0,1:T(8,128)(2,1)}, u32[]{:S(2)}, u32[]{:S(2)}) collective-permute-start(bf16[32,128,128]{2,0,1:T(8,128)(2,1)} %collective-permute-done.7), channel_id=1, source_target_pairs={{8,0},{16,8},{24,16},{28,24},{20,28},{12,20},{4,12},{0,4},{9,1},{1... | collective-permute-start | bytes 3145736 | tf_op jit(solution)/shard_map/ppermute | solution.py:60
  160.6 59.3 %copy-start.1 = (bf16[8,512,256]{2,0,1:T(8,128)(2,1)}, bf16[8,512,256]{2,0,1:T(8,128)(2,1)S(1)}, u32[]{:S(2)}) copy-start(bf16[8,512,256]{2,0,1:T(8,128)(2,1)S(1)} %fusion.17) | copy-start | bytes 6291460
  167.1 20.2 %copy-start.5 = (f32[8,64]{1,0:T(8,128)S(1)}, f32[8,64]{1,0:T(8,128)}, u32[]{:S(2)}) copy-start(f32[8,64]{1,0:T(8,128)} %param.20) | copy-start | bytes 6148
  178.4 41.3 %collective-permute-start.10 = (bf16[32,128,128]{2,0,1:T(8,128)(2,1)}, bf16[32,128,128]{2,0,1:T(8,128)(2,1)S(1)}, u32[]{:S(2)}, u32[]{:S(2)}) collective-permute-start(bf16[32,128,128]{2,0,1:T(8,128)(2,1)} %collective-permute-done.8), channel_id=1, source_target_pairs={{0,8},{8,16},{16,24},{24,28},{28,20},{20,12},{12,4},{4,0},{1,9},{9... | collective-permute-start | bytes 3145736 | tf_op jit(solution)/shard_map/ppermute | solution.py:59
  180.7 40.5 %collective-permute-start.11 = (bf16[32,128,128]{2,0,1:T(8,128)(2,1)}, bf16[32,128,128]{2,0,1:T(8,128)(2,1)}, u32[]{:S(2)}, u32[]{:S(2)}) collective-permute-start(bf16[32,128,128]{2,0,1:T(8,128)(2,1)} %collective-permute-done.9), channel_id=1, source_target_pairs={{8,0},{16,8},{24,16},{28,24},{20,28},{12,20},{4,12},{0,4},{9,1},{1... | collective-permute-start | bytes 3145736 | tf_op jit(solution)/shard_map/ppermute | solution.py:60
  187.3 45.6 %copy-start.4 = (f32[8,64]{1,0:T(8,128)}, f32[8,64]{1,0:T(8,128)S(1)}, u32[]{:S(2)}) copy-start(f32[8,64]{1,0:T(8,128)S(1)} %psum.7) | copy-start | bytes 6148
  219.7 16.9 %collective-permute-start.12 = (bf16[32,128,128]{2,0,1:T(8,128)(2,1)S(1)}, bf16[32,128,128]{2,0,1:T(8,128)(2,1)S(1)}, u32[]{:S(2)}, u32[]{:S(2)}) collective-permute-start(bf16[32,128,128]{2,0,1:T(8,128)(2,1)S(1)} %collective-permute-done.10), channel_id=1, source_target_pairs={{0,8},{8,16},{16,24},{24,28},{28,20},{20,12},{12,4},{4,0},{1,9},{9... | collective-permute-start | bytes 3145736 | tf_op jit(solution)/shard_map/ppermute | solution.py:59
  221.2 16.5 %collective-permute-start.13 = (bf16[32,128,128]{2,0,1:T(8,128)(2,1)}, bf16[32,128,128]{2,0,1:T(8,128)(2,1)S(1)}, u32[]{:S(2)}, u32[]{:S(2)}) collective-permute-start(bf16[32,128,128]{2,0,1:T(8,128)(2,1)} %collective-permute-done.11), channel_id=1, source_target_pairs={{8,0},{16,8},{24,16},{28,24},{20,28},{12,20},{4,12},{0,4},{9,1},{1... | collective-permute-start | bytes 3145736 | tf_op jit(solution)/shard_map/ppermute | solution.py:60
  251.7 6.5 %copy-start.10 = (u32[32]{0:T(128)S(1)}, u32[32]{0:T(128)}, u32[]{:S(2)}) copy-start(u32[32]{0:T(128)} %constant.39) | copy-start | bytes 388
  251.7 59.2 %copy-start.2 = (bf16[16,128,4,128]{1,0,3,2:T(8,128)(2,1)S(1)}, bf16[16,128,4,128]{1,0,3,2:T(8,128)(2,1)}, u32[]{:S(2)}) copy-start(bf16[16,128,4,128]{1,0,3,2:T(8,128)(2,1)} %copy.66) | copy-start | bytes 6291460
  258.1 108.9 %all-reduce.11.cloned.1.call-start = ((), (), s32[]{:S(2)}) async-start(), calls=%async_computation.3 | async-start | bytes 4194304
  315.4 109.5 %all-reduce.13.cloned.1.call-start = ((), (), s32[]{:S(2)}) async-start(), calls=%async_computation.4 | async-start | bytes 4194304
  373.4 109.6 %all-reduce.15.cloned.1.call-start = ((), (), s32[]{:S(2)}) async-start(), calls=%async_computation.5 | async-start | bytes 4194304
Sparse Core Ops, SparseCore 0:
  10.1 44.8 all-gather.7
  57.2 61.7 all-gather.5
  258.2 50.7 all-reduce.8
  315.5 51.4 all-reduce.10
  373.5 51.4 all-reduce.12
  431.4 51.4 all-reduce.14

commit v2 on v1

--- a/solution.py
+++ b/solution.py
@@ -1,6 +1,10 @@
+import functools
+
 import jax
 import jax.numpy as jnp
 from jax import lax
+from jax.experimental import pallas as pl
+from jax.experimental.pallas import tpu as pltpu
 from jax.sharding import PartitionSpec as P
 
 TAYLOR = 4
@@ -12,6 +16,148 @@
 def ring_order(size):
     half = size // 2
     return [2 * p for p in range(half)] + [2 * (size - 1 - p) + 1 for p in range(half, size)]
+
+
+def series_kernel(
+    pairs,
+    op_ref,
+    walk_ref,
+    out_ref,
+    op_peer,
+    walk_in,
+    term,
+    total,
+    send_buf,
+    recv_buf,
+    end_send,
+    end_recv,
+    swap_send,
+    swap_recv,
+    send_sem,
+    recv_sem,
+):
+    f32 = jnp.float32
+    bf16 = jnp.bfloat16
+    wide = lax.axis_index("wide")
+    me = lax.axis_index("chol")
+    core = me % 2
+    pair = me // 2
+    partner = me + 1 - 2 * core
+    rows = op_ref.shape[1]
+    chunks = send_buf.shape[2]
+    piece = send_buf.shape[3]
+    peers = [((pair + j) % pairs) for j in range(1, pairs)]
+
+    def place(chol):
+        return (wide, chol)
+
+    barrier = pltpu.get_barrier_semaphore()
+    for other in [partner] + [2 * p + core for p in peers]:
+        pl.semaphore_signal(
+            barrier, inc=1, device_id=place(other), device_id_type=pl.DeviceIdType.MESH
+        )
+    pl.semaphore_wait(barrier, pairs)
+
+    def remote(src, dst, send, recv, other):
+        return pltpu.make_async_remote_copy(
+            src_ref=src,
+            dst_ref=dst,
+            send_sem=send,
+            recv_sem=recv,
+            device_id=place(other),
+            device_id_type=pl.DeviceIdType.MESH,
+        )
+
+    walk_swap = remote(
+        walk_ref.at[1 - core], walk_in, swap_send.at[0], swap_recv.at[0], partner
+    )
+    op_swap = remote(op_ref, op_peer, swap_send.at[1], swap_recv.at[1], partner)
+    walk_swap.start()
+    op_swap.start()
+    own_at = pl.ds(pl.multiple_of(core * rows, rows), rows)
+    other_at = pl.ds(pl.multiple_of((1 - core) * rows, rows), rows)
+    term[own_at, :] = walk_ref[core]
+    total[own_at, :] = walk_ref[core].astype(f32)
+    walk_swap.wait()
+    term[other_at, :] = walk_in[...]
+    total[other_at, :] = walk_in[...].astype(f32)
+    op_swap.wait()
+
+    def product(start, count):
+        at = pl.ds(pl.multiple_of(start, piece), count)
+        return jnp.dot(op_ref[at, :], term[own_at, :], preferred_element_type=f32) + jnp.dot(
+            op_peer[at, :], term[other_at, :], preferred_element_type=f32
+        )
+
+    for order in range(1, TAYLOR + 1):
+        copies = []
+        for j, p in enumerate(peers):
+            for c in range(chunks):
+                slot = (order - 1, j, c)
+                send_buf[slot] = product(p * (2 * rows) + c * piece, piece).astype(bf16)
+                copy = remote(
+                    send_buf.at[slot],
+                    recv_buf.at[slot],
+                    send_sem.at[slot],
+                    recv_sem.at[slot],
+                    2 * p + core,
+                )
+                copy.start()
+                copies.append(copy)
+        parts = [product(pair * (2 * rows) + c * piece, piece) for c in range(chunks)]
+        for c in range(chunks):
+            part = parts[c]
+            for j in range(len(peers)):
+                copies[j * chunks + c].wait()
+                part = part + recv_buf[order - 1, j, c].astype(f32)
+            parts[c] = (SQRT_TAU / order * part).astype(bf16)
+        for c in range(chunks):
+            at = pl.ds(c * piece, piece)
+            term[at, :] = parts[c]
+            total[at, :] += parts[c].astype(f32)
+    end_send[...] = total[other_at, :].astype(bf16)
+    end_swap = remote(end_send, end_recv, swap_send.at[2], swap_recv.at[2], partner)
+    end_swap.start()
+    out_ref[core] = total[own_at, :].astype(bf16)
+    end_swap.wait()
+    out_ref[1 - core] = end_recv[...]
+
+
+def taylor(own_op, own_walkers, chol):
+    bf16 = jnp.bfloat16
+    orbitals, rows = own_op.shape
+    electrons = own_walkers.shape[1]
+    half = electrons // 2
+    pairs = chol // 2
+    chunks = 4
+    piece = 2 * rows // chunks
+    others = max(pairs - 1, 1)
+    slots = (TAYLOR, others, chunks)
+    walk = jnp.transpose(own_walkers.reshape(rows, 2, half), (1, 0, 2))
+    out = pl.pallas_call(
+        functools.partial(series_kernel, pairs),
+        out_shape=jax.ShapeDtypeStruct((2, rows, half), bf16),
+        in_specs=[pl.BlockSpec(memory_space=pltpu.VMEM)] * 2,
+        out_specs=pl.BlockSpec(memory_space=pltpu.VMEM),
+        scratch_shapes=[
+            pltpu.VMEM((orbitals, rows), bf16),
+            pltpu.VMEM((rows, half), bf16),
+            pltpu.VMEM((2 * rows, half), bf16),
+            pltpu.VMEM((2 * rows, half), jnp.float32),
+            pltpu.VMEM(slots + (piece, half), bf16),
+            pltpu.VMEM(slots + (piece, half), bf16),
+            pltpu.VMEM((rows, half), bf16),
+            pltpu.VMEM((rows, half), bf16),
+            pltpu.SemaphoreType.DMA((3,)),
+            pltpu.SemaphoreType.DMA((3,)),
+            pltpu.SemaphoreType.DMA(slots),
+            pltpu.SemaphoreType.DMA(slots),
+        ],
+        compiler_params=pltpu.CompilerParams(
+            collective_id=0, has_side_effects=True, vmem_limit_bytes=32 * 1024 * 1024
+        ),
+    )(own_op, walk)
+    return jnp.transpose(out, (1, 0, 2)).reshape(rows, electrons)
 
 
 def body(
@@ -114,16 +260,8 @@
         preferred_element_type=f32,
     ).astype(bf16)
     own_op = spread.reshape(1, orbitals, orb_rows)
-    term = own_walkers
-    total = own_walkers.astype(f32)
-    for order in range(1, TAYLOR + 1):
-        product = jnp.einsum("wpm,wmn->pwn", own_op, term, preferred_element_type=f32)
-        summed = lax.psum_scatter(
-            product.astype(bf16), "chol", scatter_dimension=0, tiled=True
-        ).astype(f32)
-        term = (SQRT_TAU / order * jnp.transpose(summed, (1, 0, 2))).astype(bf16)
-        total = total + term.astype(f32)
-    return (force_bias, total.astype(bf16))
+    total = taylor(own_op[0], own_walkers[0], lax.axis_size("chol"))
+    return (force_bias, total[None])
 
 
 def solution(mesh):

time: 496 us -> 295 us (0.59)
  waiting for transfers between devices: 269 us -> 56.5 us
  Pallas kernels: 0 us -> 36.2 us
  local copies, waits for them, and re-layouts: 62.5 us -> 51.2 us
  other arithmetic: 10.6 us -> 2.07 us
    unnamed x10 -> x2, waiting for transfers between devices: 205 us -> 0.7 us
    pallas_call x0 -> x1, Pallas kernels: none -> 36.2 us  [taylor(): pl.pallas_call(functools.partial(series_kernel, pairs), out_shape=jax.Sha...]
    convert_element_type x4 -> x0, local copies, waits for them, and re-layouts: 15.2 us -> none  [body(): product.astype(bf16)]
    convert_element_type x4 -> x0, other arithmetic: 9.87 us -> none  [the longest x3 5.28 us: body(): term = (SQRT_TAU / order * jnp.transpose(summed, (1, 0, 2))).astype(bf16)]
    ppermute x7, waiting for transfers between devices: 58.5 us -> 52.5 us  [body(): going = lax.ppermute(going, 'wide', right)]
    unnamed x41 -> x31, local copies, waits for them, and re-layouts: 33.2 us -> 38.9 us
  transfers between devices with their start and end apart: 20 -> 16, of which waited for: 9 -> 5; matrix products, arithmetic and copies ran while one was open for 12% -> 23% of each run, Pallas kernels for 0% -> 0%
where the time goes in v2:
time: 295 us; the launch traced here: 294 us
  blocking collectives  79.1 us (27%)
  waiting for transfers between devices  56.5 us (19%)
  local copies, waits for them, and re-layouts  51.2 us (17%)
  Pallas kernels  36.2 us (12%)
  matrix products  27.6 us (9%)
  starting transfers between devices  26.2 us (9%)
  between operations  15 us (5%)
    ppermute x7, waiting for transfers between devices, body(): going = lax.ppermute(going, 'wide', right)  52.5 us
    all_gather x1, blocking collectives, body(): meta = lax.all_gather(jnp.stack([place_own, tile_vector]), 'wide', axis=0)  42.3 us
    unnamed x31, local copies, waits for them, and re-layouts  38.9 us
    pallas_call x1, Pallas kernels, taylor(): pl.pallas_call(functools.partial(series_kernel, pairs), out_shape=jax.Sha...  36.2 us
    all_gather x1, blocking collectives, body(): field_all = lax.all_gather(field, 'wide', axis=0)  30.7 us
    ppermute x7, starting transfers between devices, body(): going = lax.ppermute(going, 'wide', right)  13.2 us
    ppermute x7, starting transfers between devices, body(): coming = lax.ppermute(coming, 'wide', left)  13 us
    dot_general x1, matrix products, body(): jnp.einsum('akt,tpq->apkq', weights_in.reshape(row_blocks, col_blocks, -1...  8.88 us
  transfers between devices with their start and end apart: 16, of which 5 were waited for; matrix products, arithmetic and copies ran while one was open for 23% of the time, Pallas kernels for 0%

profile of v2, /device:TPU:0, one launch (start us, length us, event | category | flops | bytes accessed | tf_op | source)
XLA Modules:
  0.0 293.9 jit_solution(17802334438615378439)
XLA Ops:
  7.2 0.7 all-gather.8.cloned.1.call-update
  8.0 1.7 fusion.48
  9.6 1.7 copy.94
  11.3 3.0 %collective-permute-start = (bf16[32,128,128]{2,0,1:T(8,128)(2,1)}, bf16[32,128,128]{2,0,1:T(8,128)(2,1)}, u32[]{:S(2)}, u32[]{:S(2)}) collective-permute-start(bf16[32,128,128]{2,0,1:T(8,128)(2,1)} %copy.94), channel_id=1, source_target_pairs={{0,8},{8,16},{16,24},{24,28},{28,20},{20,12},{12,4},{4,0},{1,9},{9... | collective-permute-start | bytes 3145736 | tf_op jit(solution)/shard_map/ppermute | solution.py:205
  14.4 0.7 copy.95
  15.8 0.7 fusion.46
  16.5 0.7 add_bitcast_fusion
  17.1 42.3 %all-gather.2 = s32[8,2,64]{2,1,0:T(2,128)S(1)} all-gather(s32[1,2,64]{2,1,0:T(2,128)S(1)} %add_bitcast_fusion), channel_id=2, replica_groups=mesh['wide'=8,'chol'=4] {'wide'}, dimensions={0}, use_global_device_ids=true | all-gather | bytes 4608 | tf_op jit(solution)/shard_map/all_gather | solution.py:188
  59.4 0.7 fusion.45
  60.1 2.4 collective-permute-start.3
  62.8 1.6 reshape.100
  64.6 1.9 convolution_convert_fusion
  66.5 28.1 %collective-permute-done.2 = bf16[32,128,128]{2,0,1:T(8,128)(2,1)} collective-permute-done((bf16[32,128,128]{2,0,1:T(8,128)(2,1)}, bf16[32,128,128]{2,0,1:T(8,128)(2,1)}, u32[]{:S(2)}, u32[]{:S(2)}) %collective-permute-start.2) | collective-permute-done | bytes 1048608 | tf_op jit(solution)/shard_map/ppermute | solution.py:205
  94.7 2.5 collective-permute-start.4
  97.1 3.3 %collective-permute-done.3 = bf16[32,128,128]{2,0,1:T(8,128)(2,1)} collective-permute-done((bf16[32,128,128]{2,0,1:T(8,128)(2,1)}, bf16[32,128,128]{2,0,1:T(8,128)(2,1)}, u32[]{:S(2)}, u32[]{:S(2)}) %collective-permute-start.3) | collective-permute-done | bytes 1048608 | tf_op jit(solution)/shard_map/ppermute | solution.py:206
  100.5 5.0 %collective-permute-start.5 = (bf16[32,128,128]{2,0,1:T(8,128)(2,1)}, bf16[32,128,128]{2,0,1:T(8,128)(2,1)}, u32[]{:S(2)}, u32[]{:S(2)}) collective-permute-start(bf16[32,128,128]{2,0,1:T(8,128)(2,1)} %collective-permute-done.3), channel_id=1, source_target_pairs={{8,0},{16,8},{24,16},{28,24},{20,28},{12,20},{4,12},{0,4},{9,1},{1... | collective-permute-start | bytes 3145736 | tf_op jit(solution)/shard_map/ppermute | solution.py:206
  105.5 1.1 copy.68
  106.6 2.7 constant_dynamic-update-slice_fusion.14
  109.3 3.3 %convert_bitcast_fusion = bf16[64,128,256]{1,2,0:T(8,128)(2,1)} fusion(bf16[64,128,256]{2,1,0:T(8,128)(2,1)S(1)} %bitcast.78, bf16[64,128,128]{2,1,0:T(8,128)(2,1)S(1)} %copy-done), kind=kOutput, calls=%fused_computation.6 | convolution fusion | flops 538968064 | bytes 10485760 | tf_op jit(solution)/shard_map/tpq,tpn->tqn/dot_general | solution.py:222
  112.6 17.3 %collective-permute-done.4 = bf16[32,128,128]{2,0,1:T(8,128)(2,1)} collective-permute-done((bf16[32,128,128]{2,0,1:T(8,128)(2,1)}, bf16[32,128,128]{2,0,1:T(8,128)(2,1)}, u32[]{:S(2)}, u32[]{:S(2)}) %collective-permute-start.4) | collective-permute-done | bytes 1048608 | tf_op jit(solution)/shard_map/ppermute | solution.py:205
  129.9 2.5 collective-permute-start.6
  132.4 1.0 collective-permute-start.7
  133.4 2.4 constant_dynamic-update-slice_fusion.13
  135.8 2.4 constant_dynamic-update-slice_fusion.12
  138.2 2.0 convolution_convert_fusion.1
  140.2 2.4 constant_dynamic-update-slice_fusion.11
  142.6 2.4 constant_dynamic-update-slice_fusion.10
  145.1 2.5 constant_dynamic-update-slice_fusion.9
  147.5 2.4 constant_dynamic-update-slice_fusion.8
  150.0 3.1 %collective-permute-done.6 = bf16[32,128,128]{2,0,1:T(8,128)(2,1)} collective-permute-done((bf16[32,128,128]{2,0,1:T(8,128)(2,1)}, bf16[32,128,128]{2,0,1:T(8,128)(2,1)}, u32[]{:S(2)}, u32[]{:S(2)}) %collective-permute-start.6) | collective-permute-done | bytes 1048608 | tf_op jit(solution)/shard_map/ppermute | solution.py:205
  153.0 2.5 collective-permute-start.8
  155.5 1.2 collective-permute-start.9
  156.7 2.9 fusion.9
  159.6 2.1 fusion.12
  161.7 4.3 %copy.53 = bf16[8,4,128,256]{2,0,3,1:T(8,128)(2,1)} copy(bf16[8,4,128,256]{3,2,1,0:T(8,128)(2,1)} %bitcast.80) | data formatting | bytes 4194304 | tf_op jit(solution)/shard_map/reshape | solution.py:225
  166.0 6.4 %fusion.23 = f32[8,64]{1,0:T(8,128)S(1)} fusion(bf16[8,4,128,256]{2,0,3,1:T(8,128)(2,1)} %copy.53, bf16[64,128,256]{1,2,0:T(8,128)(2,1)} %convert_bitcast_fusion, f32[64,4]{0,1:T(4,128)S(1)} %fusion.44), kind=kOutput, calls=%fused_computation.18 | convolution fusion | flops 134221312 | bytes 6294528 | tf_op jit(solution)/shard_map/tqn,wcqn->wtc/dot_general | solution.py:226
  172.4 4.0 %collective-permute-done.8 = bf16[32,128,128]{2,0,1:T(8,128)(2,1)} collective-permute-done((bf16[32,128,128]{2,0,1:T(8,128)(2,1)}, bf16[32,128,128]{2,0,1:T(8,128)(2,1)}, u32[]{:S(2)}, u32[]{:S(2)}) %collective-permute-start.8) | collective-permute-done | bytes 1048608 | tf_op jit(solution)/shard_map/ppermute | solution.py:205
  176.4 2.5 collective-permute-start.10
  178.8 1.2 collective-permute-start.11
  180.0 0.2 fusion.34
  180.2 6.0 %psum.7 = f32[8,64]{1,0:T(8,128)S(1)} all-reduce(f32[8,64]{1,0:T(8,128)S(1)} %fusion.34), channel_id=1, replica_groups=mesh['wide'=8,'chol'=4] {'chol'}, use_global_device_ids=true, to_apply=%region_1.2 | all-reduce | flops 512 | bytes 4096 | tf_op jit(solution)/shard_map/psum | solution.py:229
  186.3 30.7 %all-gather.1 = bf16[64,64]{1,0:T(8,128)(2,1)S(1)} all-gather(bf16[8,64]{1,0:T(8,128)(2,1)S(1)} %subtract_convert_fusion), channel_id=3, replica_groups=mesh['wide'=8,'chol'=4] {'wide'}, dimensions={0}, use_global_device_ids=true | all-gather | bytes 9216 | tf_op jit(solution)/shard_map/all_gather | solution.py:231
  217.0 0.3 select_reduce_fusion
  217.3 0.1 select_reduce_fusion.1
  217.4 0.1 slice.39
  217.7 0.2 collective-permute-start.12
  217.9 0.5 constant_dynamic-slice_fusion
  218.4 0.7 copy.61
  219.1 0.2 copy.62
  219.3 2.1 collective-permute-start.13
  221.5 2.4 constant_dynamic-update-slice_fusion.7
  223.9 2.4 constant_dynamic-update-slice_fusion.6
  226.3 2.5 constant_dynamic-update-slice_fusion.5
  228.8 2.4 constant_dynamic-update-slice_fusion.4
  231.2 2.4 constant_dynamic-update-slice_fusion.3
  233.6 2.4 constant_dynamic-update-slice_fusion.2
  236.0 2.4 constant_dynamic-update-slice_fusion.1
  238.4 1.2 constant_dynamic-update-slice_fusion
  239.6 8.9 %convert_bitcast_fusion.1 = bf16[16,128,4,128]{3,0,2,1:T(8,128)(2,1)S(1)} fusion(bf16[512,128,128]{2,0,1:T(8,128)(2,1)} %constant_dynamic-update-slice_fusion, bf16[512]{0:T(512)(128)(2,1)S(1)} %pad_maximum_fusion.1, s32[16,4]{0,1:T(4,128)S(1)} %multiply_add_fusion, s32[512]{0:T(512)S(1)} %pad_add_fusion.1), kind=kOutput, calls=%fused_computation.12 | convolution fusion | flops 1074855936 | bytes 18877696 | tf_op jit(solution)/shard_map/akt,tpq->apkq/dot_general | solution.py:256
  248.5 1.0 copy.60
  249.5 0.4 copy.96
  249.9 36.2 %shard_map.122 = bf16[2,512,128]{2,1,0:T(8,128)(2,1)S(1)} custom-call(bf16[2048,512]{1,0:T(8,128)(2,1)S(1)} %bitcast.74, bf16[2,512,128]{2,1,0:T(8,128)(2,1)S(1)} %bitcast.75), custom_call_target="tpu_custom_call" | custom-call | tf_op jit(solution)/shard_map/pallas_call | solution.py:137
  286.0 0.1 copy.63
  286.2 0.8 copy.64
  (49 shorter events, 0.9 us)
Async XLA Ops:
  7.2 99.5 %copy-start = (bf16[64,128,128]{2,1,0:T(8,128)(2,1)S(1)}, bf16[64,128,128]{2,1,0:T(8,128)(2,1)}, u32[]{:S(2)}) copy-start(bf16[64,128,128]{2,1,0:T(8,128)(2,1)} %param.14) | copy-start | bytes 6291460
  7.2 99.4 %copy-start.4 = (s32[64]{0:T(128)S(1)}, s32[64]{0:T(128)}, u32[]{:S(2)}) copy-start(s32[64]{0:T(128)} %param.17) | copy-start | bytes 772
  7.2 131.0 %all-gather.8.cloned.1.call-start = ((), (), s32[]{:S(2)}) async-start(), calls=%async_computation.1 | async-start | bytes 1179648 | tf_op jit(solution)/shard_map/all_gather | solution.py:190
  7.9 148.8 %all-gather.6.cloned.1.call-start = ((), (), s32[]{:S(2)}) async-start(), calls=%async_computation | async-start | bytes 2359296 | tf_op jit(solution)/shard_map/all_gather | solution.py:189
  11.3 48.7 %collective-permute-start = (bf16[32,128,128]{2,0,1:T(8,128)(2,1)}, bf16[32,128,128]{2,0,1:T(8,128)(2,1)}, u32[]{:S(2)}, u32[]{:S(2)}) collective-permute-start(bf16[32,128,128]{2,0,1:T(8,128)(2,1)} %copy.94), channel_id=1, source_target_pairs={{0,8},{8,16},{16,24},{24,28},{28,20},{20,12},{12,4},{4,0},{1,9},{9... | collective-permute-start | bytes 3145736 | tf_op jit(solution)/shard_map/ppermute | solution.py:205
  15.0 45.0 %collective-permute-start.1 = (bf16[32,128,128]{2,0,1:T(8,128)(2,1)S(1)}, bf16[32,128,128]{2,0,1:T(8,128)(2,1)}, u32[]{:S(2)}, u32[]{:S(2)}) collective-permute-start(bf16[32,128,128]{2,0,1:T(8,128)(2,1)S(1)} %copy.95), channel_id=1, source_target_pairs={{8,0},{16,8},{24,16},{28,24},{20,28},{12,20},{4,12},{0,4},{9,1},{1... | collective-permute-start | bytes 3145736 | tf_op jit(solution)/shard_map/ppermute | solution.py:206
  60.1 34.6 %collective-permute-start.2 = (bf16[32,128,128]{2,0,1:T(8,128)(2,1)}, bf16[32,128,128]{2,0,1:T(8,128)(2,1)}, u32[]{:S(2)}, u32[]{:S(2)}) collective-permute-start(bf16[32,128,128]{2,0,1:T(8,128)(2,1)} %collective-permute-done), channel_id=1, source_target_pairs={{0,8},{8,16},{16,24},{24,28},{28,20},{20,12},{12,4},{4,0},{1,9},{9... | collective-permute-start | bytes 3145736 | tf_op jit(solution)/shard_map/ppermute | solution.py:205
  60.1 40.4 %collective-permute-start.3 = (bf16[32,128,128]{2,0,1:T(8,128)(2,1)}, bf16[32,128,128]{2,0,1:T(8,128)(2,1)}, u32[]{:S(2)}, u32[]{:S(2)}) collective-permute-start(bf16[32,128,128]{2,0,1:T(8,128)(2,1)} %collective-permute-done.1), channel_id=1, source_target_pairs={{8,0},{16,8},{24,16},{28,24},{20,28},{12,20},{4,12},{0,4},{9,1},{1... | collective-permute-start | bytes 3145736 | tf_op jit(solution)/shard_map/ppermute | solution.py:206
  64.4 73.8 %copy-start.3 = (s32[8]{0:T(128)S(1)}, s32[8]{0:T(128)}, u32[]{:S(2)}) copy-start(s32[8]{0:T(128)} %param.19) | copy-start | bytes 100
  94.7 35.2 %collective-permute-start.4 = (bf16[32,128,128]{2,0,1:T(8,128)(2,1)}, bf16[32,128,128]{2,0,1:T(8,128)(2,1)}, u32[]{:S(2)}, u32[]{:S(2)}) collective-permute-start(bf16[32,128,128]{2,0,1:T(8,128)(2,1)} %collective-permute-done.2), channel_id=1, source_target_pairs={{0,8},{8,16},{16,24},{24,28},{28,20},{20,12},{12,4},{4,0},{1,9},{9... | collective-permute-start | bytes 3145736 | tf_op jit(solution)/shard_map/ppermute | solution.py:205
  100.5 31.9 %collective-permute-start.5 = (bf16[32,128,128]{2,0,1:T(8,128)(2,1)}, bf16[32,128,128]{2,0,1:T(8,128)(2,1)}, u32[]{:S(2)}, u32[]{:S(2)}) collective-permute-start(bf16[32,128,128]{2,0,1:T(8,128)(2,1)} %collective-permute-done.3), channel_id=1, source_target_pairs={{8,0},{16,8},{24,16},{28,24},{20,28},{12,20},{4,12},{0,4},{9,1},{1... | collective-permute-start | bytes 3145736 | tf_op jit(solution)/shard_map/ppermute | solution.py:206
  129.9 23.1 %collective-permute-start.6 = (bf16[32,128,128]{2,0,1:T(8,128)(2,1)}, bf16[32,128,128]{2,0,1:T(8,128)(2,1)}, u32[]{:S(2)}, u32[]{:S(2)}) collective-permute-start(bf16[32,128,128]{2,0,1:T(8,128)(2,1)} %collective-permute-done.4), channel_id=1, source_target_pairs={{0,8},{8,16},{16,24},{24,28},{28,20},{20,12},{12,4},{4,0},{1,9},{9... | collective-permute-start | bytes 3145736 | tf_op jit(solution)/shard_map/ppermute | solution.py:205
  132.4 23.1 %collective-permute-start.7 = (bf16[32,128,128]{2,0,1:T(8,128)(2,1)}, bf16[32,128,128]{2,0,1:T(8,128)(2,1)}, u32[]{:S(2)}, u32[]{:S(2)}) collective-permute-start(bf16[32,128,128]{2,0,1:T(8,128)(2,1)} %collective-permute-done.5), channel_id=1, source_target_pairs={{8,0},{16,8},{24,16},{28,24},{20,28},{12,20},{4,12},{0,4},{9,1},{1... | collective-permute-start | bytes 3145736 | tf_op jit(solution)/shard_map/ppermute | solution.py:206
  138.2 41.8 %copy-start.5 = (s32[64]{0:T(128)S(1)}, s32[64]{0:T(128)}, u32[]{:S(2)}) copy-start(s32[64]{0:T(128)} %param.15) | copy-start | bytes 772
  138.2 48.1 %copy-start.2 = (f32[8,64]{1,0:T(8,128)S(1)}, f32[8,64]{1,0:T(8,128)}, u32[]{:S(2)}) copy-start(f32[8,64]{1,0:T(8,128)} %param.20) | copy-start | bytes 6148
  153.0 23.3 %collective-permute-start.8 = (bf16[32,128,128]{2,0,1:T(8,128)(2,1)}, bf16[32,128,128]{2,0,1:T(8,128)(2,1)}, u32[]{:S(2)}, u32[]{:S(2)}) collective-permute-start(bf16[32,128,128]{2,0,1:T(8,128)(2,1)} %collective-permute-done.6), channel_id=1, source_target_pairs={{0,8},{8,16},{16,24},{24,28},{28,20},{20,12},{12,4},{4,0},{1,9},{9... | collective-permute-start | bytes 3145736 | tf_op jit(solution)/shard_map/ppermute | solution.py:205
  155.5 23.3 %collective-permute-start.9 = (bf16[32,128,128]{2,0,1:T(8,128)(2,1)}, bf16[32,128,128]{2,0,1:T(8,128)(2,1)}, u32[]{:S(2)}, u32[]{:S(2)}) collective-permute-start(bf16[32,128,128]{2,0,1:T(8,128)(2,1)} %collective-permute-done.7), channel_id=1, source_target_pairs={{8,0},{16,8},{24,16},{28,24},{20,28},{12,20},{4,12},{0,4},{9,1},{1... | collective-permute-start | bytes 3145736 | tf_op jit(solution)/shard_map/ppermute | solution.py:206
  176.4 41.3 %collective-permute-start.10 = (bf16[32,128,128]{2,0,1:T(8,128)(2,1)}, bf16[32,128,128]{2,0,1:T(8,128)(2,1)}, u32[]{:S(2)}, u32[]{:S(2)}) collective-permute-start(bf16[32,128,128]{2,0,1:T(8,128)(2,1)} %collective-permute-done.8), channel_id=1, source_target_pairs={{0,8},{8,16},{16,24},{24,28},{28,20},{20,12},{12,4},{4,0},{1,9},{9... | collective-permute-start | bytes 3145736 | tf_op jit(solution)/shard_map/ppermute | solution.py:205
  178.8 40.4 %collective-permute-start.11 = (bf16[32,128,128]{2,0,1:T(8,128)(2,1)}, bf16[32,128,128]{2,0,1:T(8,128)(2,1)}, u32[]{:S(2)}, u32[]{:S(2)}) collective-permute-start(bf16[32,128,128]{2,0,1:T(8,128)(2,1)} %collective-permute-done.9), channel_id=1, source_target_pairs={{8,0},{16,8},{24,16},{28,24},{20,28},{12,20},{4,12},{0,4},{9,1},{1... | collective-permute-start | bytes 3145736 | tf_op jit(solution)/shard_map/ppermute | solution.py:206
  186.3 62.2 %copy-start.1 = (f32[8,64]{1,0:T(8,128)}, f32[8,64]{1,0:T(8,128)S(1)}, u32[]{:S(2)}) copy-start(f32[8,64]{1,0:T(8,128)S(1)} %psum.7) | copy-start | bytes 6148
  217.7 18.3 %collective-permute-start.12 = (bf16[32,128,128]{2,0,1:T(8,128)(2,1)}, bf16[32,128,128]{2,0,1:T(8,128)(2,1)}, u32[]{:S(2)}, u32[]{:S(2)}) collective-permute-start(bf16[32,128,128]{2,0,1:T(8,128)(2,1)} %collective-permute-done.10), channel_id=1, source_target_pairs={{0,8},{8,16},{16,24},{24,28},{28,20},{20,12},{12,4},{4,0},{1,9},{9... | collective-permute-start | bytes 3145736 | tf_op jit(solution)/shard_map/ppermute | solution.py:205
  219.3 19.1 %collective-permute-start.13 = (bf16[32,128,128]{2,0,1:T(8,128)(2,1)}, bf16[32,128,128]{2,0,1:T(8,128)(2,1)S(1)}, u32[]{:S(2)}, u32[]{:S(2)}) collective-permute-start(bf16[32,128,128]{2,0,1:T(8,128)(2,1)} %collective-permute-done.11), channel_id=1, source_target_pairs={{8,0},{16,8},{24,16},{28,24},{20,28},{12,20},{4,12},{0,4},{9,1},{1... | collective-permute-start | bytes 3145736 | tf_op jit(solution)/shard_map/ppermute | solution.py:206
Sparse Core Ops, SparseCore 0:
  10.1 44.8 all-gather.7
  57.2 61.5 all-gather.5

commit v3 on v2

--- a/solution.py
+++ b/solution.py
@@ -184,8 +184,7 @@
     wide = lax.axis_size("wide")
     me = lax.axis_index("wide")
     live_slot = jnp.arange(slot_count, dtype=jnp.int32) < tile_count[0]
-    place_own = jnp.where(live_slot, tile_row * col_blocks + tile_col, -1)
-    meta = lax.all_gather(jnp.stack([place_own, tile_vector]), "wide", axis=0)
+    place_own = tile_row * col_blocks + tile_col
     walker_rows = lax.all_gather(walkers, "wide", axis=0, tiled=True)
     inv_all = lax.all_gather(intersection_inv, "wide", axis=0, tiled=True)
     order = ring_order(wide)
@@ -198,13 +197,6 @@
     owners = jnp.asarray(
         [[order[(spot_of[idx] + turn) % wide] for turn in turns] for idx in range(wide)], jnp.int32
     )[me]
-    half = slot_count // 2
-    going, coming = chol_tiles[:half], chol_tiles[half:]
-    parts = [chol_tiles]
-    for step in range(1, wide):
-        going = lax.ppermute(going, "wide", right)
-        coming = lax.ppermute(coming, "wide", left)
-        parts += [going, coming]
     picker = (sources[:, None] == jnp.arange(walk_all, dtype=jnp.int32)[None, :]).astype(bf16)
     picked = jnp.einsum("jw,wmn->jmn", picker, walker_rows, preferred_element_type=f32).astype(bf16)
     picked_inv = jnp.einsum("jw,wnk->jnk", picker, inv_all, preferred_element_type=f32).astype(bf16)
@@ -226,14 +218,23 @@
     scores = jnp.einsum("tqn,wcqn->wtc", projected, theta_blocks, preferred_element_type=f32)
     scores = jnp.sum(scores * col_hot[None], axis=2) * live[None, :]
     bias_part = jnp.dot(scores, vec_hot, precision=highest)
+    half = slot_count // 2
+    going, coming = chol_tiles[:half], chol_tiles[half:]
+    parts = [chol_tiles]
+    for step in range(1, wide):
+        if step == wide - 1:
+            going, coming, bias_part = lax.optimization_barrier((going, coming, bias_part))
+        going = lax.ppermute(going, "wide", right)
+        coming = lax.ppermute(coming, "wide", left)
+        parts += [going, coming]
     force_bias = lax.psum(bias_part, "chol")
     field = (aux_noise - SQRT_TAU * force_bias).astype(bf16)
-    field_all = lax.all_gather(field, "wide", axis=0)
-    own_field = lax.dynamic_index_in_dim(field_all, me * walk_dev, 1, keepdims=False)
+    coeff_own = jnp.dot(field, (vec_hot * live[:, None]).T.astype(bf16), preferred_element_type=f32)
+    sent = jnp.concatenate([coeff_own.astype(bf16), place_own.astype(bf16)[None]], axis=0)
+    got = lax.all_gather(sent, "wide", axis=0).astype(f32)
+    coeff = lax.dynamic_index_in_dim(got, me * walk_dev, 1, keepdims=False)
+    place_all = got[:, walk_all].astype(jnp.int32)
     places = row_blocks * col_blocks
-    place_all, vec_all = meta[:, 0], meta[:, 1]
-    vec_hot_all = (vec_all[:, :, None] == jnp.arange(vec_dev, dtype=jnp.int32)).astype(f32)
-    coeff = jnp.sum(vec_hot_all * own_field.astype(f32)[:, None, :], axis=2)
 
     def in_parts(whole):
         picked_rows = jnp.sum(

time: 295 us -> 305 us (1.034)
  waiting for transfers between devices: 56.5 us -> 117 us
  blocking collectives: 79.1 us -> 36.1 us
  starting transfers between devices: 26.2 us -> 18 us
    ppermute x7, waiting for transfers between devices: 52.5 us -> 108 us  [body(): going = lax.ppermute(going, 'wide', right)]
    all_gather x2 -> x1, blocking collectives: 73 us -> 30.5 us  [body(): got = lax.all_gather(sent, 'wide', axis=0).astype(f32)]
    ppermute x7, starting transfers between devices: 13 us -> 2.45 us  [body(): coming = lax.ppermute(coming, 'wide', left)]
    ppermute x7, waiting for transfers between devices: 3.33 us -> 7.91 us  [body(): coming = lax.ppermute(coming, 'wide', left)]
    unnamed x31 -> x33, local copies, waits for them, and re-layouts: 38.9 us -> 38.3 us
  transfers between devices with their start and end apart: 16 -> 16, of which waited for: 5 -> 13; matrix products, arithmetic and copies ran while one was open for 23% -> 23% of each run, Pallas kernels for 0% -> 0%
where the time goes in v3:
time: 305 us; the launch traced here: 304 us
  waiting for transfers between devices  117 us (38%)
  local copies, waits for them, and re-layouts  50.7 us (17%)
  blocking collectives  36.1 us (12%)
  Pallas kernels  35.9 us (12%)
  matrix products  30 us (10%)
  starting transfers between devices  18 us (6%)
  between operations  14.9 us (5%)
    ppermute x7, waiting for transfers between devices, body(): going = lax.ppermute(going, 'wide', right)  108 us
    unnamed x33, local copies, waits for them, and re-layouts  38.3 us
    pallas_call x1, Pallas kernels, taylor(): pl.pallas_call(functools.partial(series_kernel, pairs), out_shape=jax.Sha...  35.9 us
    all_gather x1, blocking collectives, body(): got = lax.all_gather(sent, 'wide', axis=0).astype(f32)  30.5 us
    ppermute x7, starting transfers between devices, body(): going = lax.ppermute(going, 'wide', right)  15.5 us
    dot_general x1, matrix products, body(): jnp.einsum('akt,tpq->apkq', weights_in.reshape(row_blocks, col_blocks, -1...  8.88 us
    ppermute x7, waiting for transfers between devices, body(): coming = lax.ppermute(coming, 'wide', left)  7.91 us
    dot_general x1, matrix products, body(): jnp.einsum('tqn,wcqn->wtc', projected, theta_blocks, preferred_element_ty...  6.41 us
  transfers between devices with their start and end apart: 16, of which 13 were waited for; matrix products, arithmetic and copies ran while one was open for 23% of the time, Pallas kernels for 0%

profile of v3, /device:TPU:0, one launch (start us, length us, event | category | flops | bytes accessed | tf_op | source)
XLA Modules:
  0.0 303.7 jit_solution(5780436606625191543)
XLA Ops:
  7.2 0.7 all-gather.7.cloned.1.call-update
  8.0 1.7 fusion.53
  9.6 1.7 copy.94
  11.3 3.0 collective-permute-start
  14.3 0.7 copy.95
  15.1 29.0 %collective-permute-done = bf16[32,128,128]{2,0,1:T(8,128)(2,1)} collective-permute-done((bf16[32,128,128]{2,0,1:T(8,128)(2,1)}, bf16[32,128,128]{2,0,1:T(8,128)(2,1)}, u32[]{:S(2)}, u32[]{:S(2)}) %collective-permute-start) | collective-permute-done | bytes 1048608 | tf_op jit(solution)/shard_map/ppermute | solution.py:227
  44.1 2.5 collective-permute-start.1
  46.6 1.2 collective-permute-done.6
  47.8 1.6 reshape.110
  50.0 0.7 fusion.48
  50.7 1.9 convolution_convert_fusion
  52.6 25.8 %collective-permute-done.1 = bf16[32,128,128]{2,0,1:T(8,128)(2,1)} collective-permute-done((bf16[32,128,128]{2,0,1:T(8,128)(2,1)}, bf16[32,128,128]{2,0,1:T(8,128)(2,1)}, u32[]{:S(2)}, u32[]{:S(2)}) %collective-permute-start.1) | collective-permute-done | bytes 1048608 | tf_op jit(solution)/shard_map/ppermute | solution.py:227
  78.5 2.5 collective-permute-start.2
  81.0 0.4 collective-permute-done.7
  81.3 0.7 fusion.49
  82.0 3.1 %copy.68 = bf16[8,8,128,256]{3,2,1,0:T(8,128)(2,1)} copy(bf16[8,8,128,256]{3,1,2,0:T(8,128)(2,1)S(1)} %bitcast.73) | data formatting | bytes 8388608
  85.2 2.7 constant_dynamic-update-slice_fusion.14
  87.8 5.4 %convert_bitcast_fusion = bf16[64,128,256]{1,2,0:T(8,128)(2,1)} fusion(bf16[64,128,256]{2,1,0:T(8,128)(2,1)} %bitcast.74, bf16[64,128,128]{2,1,0:T(8,128)(2,1)S(1)} %copy-done), kind=kOutput, calls=%fused_computation.6 | convolution fusion | flops 538968064 | bytes 10485760 | tf_op jit(solution)/shard_map/tpq,tpn->tqn/dot_general | solution.py:214
  93.3 24.7 %collective-permute-done.2 = bf16[32,128,128]{2,0,1:T(8,128)(2,1)} collective-permute-done((bf16[32,128,128]{2,0,1:T(8,128)(2,1)}, bf16[32,128,128]{2,0,1:T(8,128)(2,1)}, u32[]{:S(2)}, u32[]{:S(2)}) %collective-permute-start.2) | collective-permute-done | bytes 1048608 | tf_op jit(solution)/shard_map/ppermute | solution.py:227
  118.0 2.9 collective-permute-start.3
  120.9 1.8 collective-permute-done.8
  122.7 2.5 constant_dynamic-update-slice_fusion.13
  125.1 2.4 constant_dynamic-update-slice_fusion.12
  127.5 1.9 convolution_convert_fusion.1
  129.5 2.4 constant_dynamic-update-slice_fusion.11
  131.9 2.4 constant_dynamic-update-slice_fusion.10
  134.3 8.4 %collective-permute-done.3 = bf16[32,128,128]{2,0,1:T(8,128)(2,1)} collective-permute-done((bf16[32,128,128]{2,0,1:T(8,128)(2,1)}, bf16[32,128,128]{2,0,1:T(8,128)(2,1)}, u32[]{:S(2)}, u32[]{:S(2)}) %collective-permute-start.3) | collective-permute-done | bytes 1048608 | tf_op jit(solution)/shard_map/ppermute | solution.py:227
  142.7 2.2 collective-permute-start.4
  144.9 1.1 collective-permute-done.9
  146.1 2.4 constant_dynamic-update-slice_fusion.9
  148.5 2.4 constant_dynamic-update-slice_fusion.8
  150.9 2.9 fusion.9
  153.8 2.1 fusion.12
  155.9 4.3 %copy.55 = bf16[8,4,128,256]{2,0,3,1:T(8,128)(2,1)} copy(bf16[8,4,128,256]{3,2,1,0:T(8,128)(2,1)} %bitcast.76) | data formatting | bytes 4194304 | tf_op jit(solution)/shard_map/reshape | solution.py:217
  160.2 0.5 constant_dynamic-slice_fusion
  160.7 0.7 copy.61
  161.4 0.2 copy.62
  161.6 4.1 %collective-permute-done.4 = bf16[32,128,128]{2,0,1:T(8,128)(2,1)} collective-permute-done((bf16[32,128,128]{2,0,1:T(8,128)(2,1)}, bf16[32,128,128]{2,0,1:T(8,128)(2,1)}, u32[]{:S(2)}, u32[]{:S(2)}) %collective-permute-start.4) | collective-permute-done | bytes 1048608 | tf_op jit(solution)/shard_map/ppermute | solution.py:227
  165.7 2.5 collective-permute-start.5
  168.2 0.8 collective-permute-done.10
  169.0 0.3 collective-permute-start.11
  169.3 6.4 %fusion.23 = f32[8,64]{1,0:T(8,128)S(1)} fusion(bf16[8,4,128,256]{2,0,3,1:T(8,128)(2,1)} %copy.55, bf16[64,128,256]{1,2,0:T(8,128)(2,1)} %convert_bitcast_fusion, f32[64,4]{0,1:T(4,128)S(1)} %fusion.48), kind=kOutput, calls=%fused_computation.18 | convolution fusion | flops 134221312 | bytes 6294528 | tf_op jit(solution)/shard_map/tqn,wcqn->wtc/dot_general | solution.py:218
  175.7 0.2 fusion.34
  175.9 2.4 constant_dynamic-update-slice_fusion.7
  178.3 2.4 constant_dynamic-update-slice_fusion.6
  180.7 2.4 constant_dynamic-update-slice_fusion.5
  183.1 2.4 constant_dynamic-update-slice_fusion.4
  185.5 2.4 collective-permute-done.5
  188.0 2.6 collective-permute-done.11
  190.6 5.6 %psum.7 = f32[8,64]{1,0:T(8,128)S(1)} all-reduce(f32[8,64]{1,0:T(8,128)S(1)} %fusion.34), channel_id=1, replica_groups=mesh['wide'=8,'chol'=4] {'chol'}, use_global_device_ids=true, to_apply=%region_1.0 | all-reduce | flops 512 | bytes 4096 | tf_op jit(solution)/shard_map/psum | solution.py:230
  196.2 0.1 convolution_convert_fusion.2
  196.4 30.5 %all-gather.1 = bf16[8,9,64]{2,1,0:T(8,128)(2,1)S(1)} all-gather(bf16[1,9,64]{2,1,0:T(8,128)(2,1)S(1)} %maximum_bitcast_fusion), channel_id=2, replica_groups=mesh['wide'=8,'chol'=4] {'wide'}, dimensions={0}, use_global_device_ids=true | all-gather | bytes 10368 | tf_op jit(solution)/shard_map/all_gather | solution.py:234
  227.3 2.0 collective-permute-start.13
  229.7 1.2 constant_dynamic-update-slice_fusion.3
  230.9 1.2 constant_dynamic-update-slice_fusion.2
  232.1 13.8 %collective-permute-done.12 = bf16[32,128,128]{2,0,1:T(8,128)(2,1)} collective-permute-done((bf16[32,128,128]{2,0,1:T(8,128)(2,1)S(1)}, bf16[32,128,128]{2,0,1:T(8,128)(2,1)}, u32[]{:S(2)}, u32[]{:S(2)}) %collective-permute-start.12) | collective-permute-done | bytes 1048608 | tf_op jit(solution)/shard_map/ppermute | solution.py:227
  246.0 2.5 constant_dynamic-update-slice_fusion.1
  248.4 1.2 constant_dynamic-update-slice_fusion
  249.7 8.9 %convert_bitcast_fusion.1 = bf16[16,128,4,128]{3,0,2,1:T(8,128)(2,1)S(1)} fusion(bf16[512,128,128]{2,0,1:T(8,128)(2,1)} %constant_dynamic-update-slice_fusion, bf16[512]{0:T(512)(128)(2,1)S(1)} %pad_maximum_fusion.1, s32[16,4]{0,1:T(4,128)S(1)} %multiply_add_fusion, s32[512]{0:T(512)S(1)} %pad_add_fusion.1), kind=kOutput, calls=%fused_computation.12 | convolution fusion | flops 1074855936 | bytes 18877696 | tf_op jit(solution)/shard_map/akt,tpq->apkq/dot_general | solution.py:257
  258.6 1.0 copy.60
  259.6 0.4 copy.96
  259.9 35.9 %shard_map.122 = bf16[2,512,128]{2,1,0:T(8,128)(2,1)S(1)} custom-call(bf16[2048,512]{1,0:T(8,128)(2,1)S(1)} %bitcast.70, bf16[2,512,128]{2,1,0:T(8,128)(2,1)S(1)} %bitcast.71), custom_call_target="tpu_custom_call" | custom-call | tf_op jit(solution)/shard_map/pallas_call | solution.py:137
  295.8 0.1 copy.63
  296.0 0.8 copy.64
  (49 shorter events, 1.2 us)
Async XLA Ops:
  7.2 78.0 %copy-start = (bf16[64,128,128]{2,1,0:T(8,128)(2,1)S(1)}, bf16[64,128,128]{2,1,0:T(8,128)(2,1)}, u32[]{:S(2)}) copy-start(bf16[64,128,128]{2,1,0:T(8,128)(2,1)} %param.14) | copy-start | bytes 6291460
  7.2 120.4 %all-gather.7.cloned.1.call-start = ((), (), s32[]{:S(2)}) async-start(), calls=%async_computation.1 | async-start | bytes 1179648 | tf_op jit(solution)/shard_map/all_gather | solution.py:189
  7.9 142.9 %all-gather.5.cloned.1.call-start = ((), (), s32[]{:S(2)}) async-start(), calls=%async_computation | async-start | bytes 2359296 | tf_op jit(solution)/shard_map/all_gather | solution.py:188
  11.3 111.4 %copy-start.3 = (s32[64]{0:T(128)S(1)}, s32[64]{0:T(128)}, u32[]{:S(2)}) copy-start(s32[64]{0:T(128)} %param.17) | copy-start | bytes 772
  11.3 111.4 %copy-start.4 = (s32[64]{0:T(128)S(1)}, s32[64]{0:T(128)}, u32[]{:S(2)}) copy-start(s32[64]{0:T(128)} %param.16) | copy-start | bytes 772
  11.3 32.8 %collective-permute-start = (bf16[32,128,128]{2,0,1:T(8,128)(2,1)}, bf16[32,128,128]{2,0,1:T(8,128)(2,1)}, u32[]{:S(2)}, u32[]{:S(2)}) collective-permute-start(bf16[32,128,128]{2,0,1:T(8,128)(2,1)} %copy.94), channel_id=1, source_target_pairs={{0,8},{8,16},{16,24},{24,28},{28,20},{20,12},{12,4},{4,0},{1,9},{9... | collective-permute-start | bytes 3145736 | tf_op jit(solution)/shard_map/ppermute | solution.py:227
  15.0 32.7 %collective-permute-start.6 = (bf16[32,128,128]{2,0,1:T(8,128)(2,1)S(1)}, bf16[32,128,128]{2,0,1:T(8,128)(2,1)}, u32[]{:S(2)}, u32[]{:S(2)}) collective-permute-start(bf16[32,128,128]{2,0,1:T(8,128)(2,1)S(1)} %copy.95), channel_id=1, source_target_pairs={{8,0},{16,8},{24,16},{28,24},{20,28},{12,20},{4,12},{0,4},{9,1},{1... | collective-permute-start | bytes 3145736 | tf_op jit(solution)/shard_map/ppermute | solution.py:228
  44.1 34.4 %collective-permute-start.1 = (bf16[32,128,128]{2,0,1:T(8,128)(2,1)}, bf16[32,128,128]{2,0,1:T(8,128)(2,1)}, u32[]{:S(2)}, u32[]{:S(2)}) collective-permute-start(bf16[32,128,128]{2,0,1:T(8,128)(2,1)} %collective-permute-done), channel_id=1, source_target_pairs={{0,8},{8,16},{16,24},{24,28},{28,20},{20,12},{12,4},{4,0},{1,9},{9... | collective-permute-start | bytes 3145736 | tf_op jit(solution)/shard_map/ppermute | solution.py:227
  47.8 33.6 %collective-permute-start.7 = (bf16[32,128,128]{2,0,1:T(8,128)(2,1)}, bf16[32,128,128]{2,0,1:T(8,128)(2,1)}, u32[]{:S(2)}, u32[]{:S(2)}) collective-permute-start(bf16[32,128,128]{2,0,1:T(8,128)(2,1)} %collective-permute-done.6), channel_id=1, source_target_pairs={{8,0},{16,8},{24,16},{28,24},{20,28},{12,20},{4,12},{0,4},{9,1},{1... | collective-permute-start | bytes 3145736 | tf_op jit(solution)/shard_map/ppermute | solution.py:228
  49.3 78.2 %copy-start.2 = (s32[8]{0:T(128)S(1)}, s32[8]{0:T(128)}, u32[]{:S(2)}) copy-start(s32[8]{0:T(128)} %param.19) | copy-start | bytes 100
  78.5 39.5 %collective-permute-start.2 = (bf16[32,128,128]{2,0,1:T(8,128)(2,1)}, bf16[32,128,128]{2,0,1:T(8,128)(2,1)}, u32[]{:S(2)}, u32[]{:S(2)}) collective-permute-start(bf16[32,128,128]{2,0,1:T(8,128)(2,1)} %collective-permute-done.1), channel_id=1, source_target_pairs={{0,8},{8,16},{16,24},{24,28},{28,20},{20,12},{12,4},{4,0},{1,9},{9... | collective-permute-start | bytes 3145736 | tf_op jit(solution)/shard_map/ppermute | solution.py:227
  81.3 41.3 %collective-permute-start.8 = (bf16[32,128,128]{2,0,1:T(8,128)(2,1)}, bf16[32,128,128]{2,0,1:T(8,128)(2,1)}, u32[]{:S(2)}, u32[]{:S(2)}) collective-permute-start(bf16[32,128,128]{2,0,1:T(8,128)(2,1)} %collective-permute-done.7), channel_id=1, source_target_pairs={{8,0},{16,8},{24,16},{28,24},{20,28},{12,20},{4,12},{0,4},{9,1},{1... | collective-permute-start | bytes 3145736 | tf_op jit(solution)/shard_map/ppermute | solution.py:228
  118.0 24.7 %collective-permute-start.3 = (bf16[32,128,128]{2,0,1:T(8,128)(2,1)}, bf16[32,128,128]{2,0,1:T(8,128)(2,1)}, u32[]{:S(2)}, u32[]{:S(2)}) collective-permute-start(bf16[32,128,128]{2,0,1:T(8,128)(2,1)} %collective-permute-done.2), channel_id=1, source_target_pairs={{0,8},{8,16},{16,24},{24,28},{28,20},{20,12},{12,4},{4,0},{1,9},{9... | collective-permute-start | bytes 3145736 | tf_op jit(solution)/shard_map/ppermute | solution.py:227
  122.7 23.3 %collective-permute-start.9 = (bf16[32,128,128]{2,0,1:T(8,128)(2,1)}, bf16[32,128,128]{2,0,1:T(8,128)(2,1)}, u32[]{:S(2)}, u32[]{:S(2)}) collective-permute-start(bf16[32,128,128]{2,0,1:T(8,128)(2,1)} %collective-permute-done.8), channel_id=1, source_target_pairs={{8,0},{16,8},{24,16},{28,24},{20,28},{12,20},{4,12},{0,4},{9,1},{1... | collective-permute-start | bytes 3145736 | tf_op jit(solution)/shard_map/ppermute | solution.py:228
  129.5 46.2 %copy-start.6 = (s32[64]{0:T(128)S(1)}, s32[64]{0:T(128)}, u32[]{:S(2)}) copy-start(s32[64]{0:T(128)} %param.15) | copy-start | bytes 772
  142.7 23.0 %collective-permute-start.4 = (bf16[32,128,128]{2,0,1:T(8,128)(2,1)}, bf16[32,128,128]{2,0,1:T(8,128)(2,1)}, u32[]{:S(2)}, u32[]{:S(2)}) collective-permute-start(bf16[32,128,128]{2,0,1:T(8,128)(2,1)} %collective-permute-done.3), channel_id=1, source_target_pairs={{0,8},{8,16},{16,24},{24,28},{28,20},{20,12},{12,4},{4,0},{1,9},{9... | collective-permute-start | bytes 3145736 | tf_op jit(solution)/shard_map/ppermute | solution.py:227
  146.0 23.0 %collective-permute-start.10 = (bf16[32,128,128]{2,0,1:T(8,128)(2,1)}, bf16[32,128,128]{2,0,1:T(8,128)(2,1)}, u32[]{:S(2)}, u32[]{:S(2)}) collective-permute-start(bf16[32,128,128]{2,0,1:T(8,128)(2,1)} %collective-permute-done.9), channel_id=1, source_target_pairs={{8,0},{16,8},{24,16},{28,24},{20,28},{12,20},{4,12},{0,4},{9,1},{1... | collective-permute-start | bytes 3145736 | tf_op jit(solution)/shard_map/ppermute | solution.py:228
  150.8 45.4 %copy-start.5 = (f32[8,64]{1,0:T(8,128)S(1)}, f32[8,64]{1,0:T(8,128)}, u32[]{:S(2)}) copy-start(f32[8,64]{1,0:T(8,128)} %param.20) | copy-start | bytes 6148
  165.7 22.2 %collective-permute-start.5 = (bf16[32,128,128]{2,0,1:T(8,128)(2,1)}, bf16[32,128,128]{2,0,1:T(8,128)(2,1)S(1)}, u32[]{:S(2)}, u32[]{:S(2)}) collective-permute-start(bf16[32,128,128]{2,0,1:T(8,128)(2,1)} %collective-permute-done.4), channel_id=1, source_target_pairs={{0,8},{8,16},{16,24},{24,28},{28,20},{20,12},{12,4},{4,0},{1,9},{9... | collective-permute-start | bytes 3145736 | tf_op jit(solution)/shard_map/ppermute | solution.py:227
  169.0 21.6 %collective-permute-start.11 = (bf16[32,128,128]{2,0,1:T(8,128)(2,1)}, bf16[32,128,128]{2,0,1:T(8,128)(2,1)S(1)}, u32[]{:S(2)}, u32[]{:S(2)}) collective-permute-start(bf16[32,128,128]{2,0,1:T(8,128)(2,1)} %collective-permute-done.10), channel_id=1, source_target_pairs={{8,0},{16,8},{24,16},{28,24},{20,28},{12,20},{4,12},{0,4},{9,1},{1... | collective-permute-start | bytes 3145736 | tf_op jit(solution)/shard_map/ppermute | solution.py:228
  196.2 62.3 %copy-start.1 = (f32[8,64]{1,0:T(8,128)}, f32[8,64]{1,0:T(8,128)S(1)}, u32[]{:S(2)}) copy-start(f32[8,64]{1,0:T(8,128)S(1)} %psum.7) | copy-start | bytes 6148
  227.3 18.7 %collective-permute-start.12 = (bf16[32,128,128]{2,0,1:T(8,128)(2,1)S(1)}, bf16[32,128,128]{2,0,1:T(8,128)(2,1)}, u32[]{:S(2)}, u32[]{:S(2)}) collective-permute-start(bf16[32,128,128]{2,0,1:T(8,128)(2,1)S(1)} %collective-permute-done.5), channel_id=1, source_target_pairs={{0,8},{8,16},{16,24},{24,28},{28,20},{20,12},{12,4},{4,0},{1,9},{9... | collective-permute-start | bytes 3145736 | tf_op jit(solution)/shard_map/ppermute | solution.py:227
  227.3 21.1 %collective-permute-start.13 = (bf16[32,128,128]{2,0,1:T(8,128)(2,1)S(1)}, bf16[32,128,128]{2,0,1:T(8,128)(2,1)S(1)}, u32[]{:S(2)}, u32[]{:S(2)}) collective-permute-start(bf16[32,128,128]{2,0,1:T(8,128)(2,1)S(1)} %collective-permute-done.11), channel_id=1, source_target_pairs={{8,0},{16,8},{24,16},{28,24},{20,28},{12,20},{4,12},{0,4},{9,1},{1... | collective-permute-start | bytes 3145736 | tf_op jit(solution)/shard_map/ppermute | solution.py:228
Sparse Core Ops, SparseCore 0:
  10.1 46.3 all-gather.6
  58.7 63.0 all-gather.4

commit v4 on v3

--- a/solution.py
+++ b/solution.py
@@ -158,6 +158,99 @@
         ),
     )(own_op, walk)
     return jnp.transpose(out, (1, 0, 2)).reshape(rows, electrons)
+
+
+def share_kernel(
+    chol,
+    wide,
+    bias_ref,
+    noise_ref,
+    hot_ref,
+    place_ref,
+    force_ref,
+    got_ref,
+    bias_in,
+    got_in,
+    sent,
+    bias_send,
+    bias_recv,
+    got_send,
+    got_recv,
+):
+    f32 = jnp.float32
+    bf16 = jnp.bfloat16
+    at_wide = lax.axis_index("wide")
+    at_chol = lax.axis_index("chol")
+    mesh_id = pl.DeviceIdType.MESH
+    in_chol = [(at_wide, (at_chol + j) % chol) for j in range(1, chol)]
+    in_wide = [((at_wide + j) % wide, at_chol) for j in range(1, wide)]
+    barrier = pltpu.get_barrier_semaphore()
+    for peer in in_chol + in_wide:
+        pl.semaphore_signal(barrier, inc=1, device_id=peer, device_id_type=mesh_id)
+    pl.semaphore_wait(barrier, chol + wide - 2)
+    copies = []
+    for j, peer in enumerate(in_chol):
+        copy = pltpu.make_async_remote_copy(
+            src_ref=bias_ref,
+            dst_ref=bias_in.at[at_chol],
+            send_sem=bias_send.at[j],
+            recv_sem=bias_recv.at[j],
+            device_id=peer,
+            device_id_type=mesh_id,
+        )
+        copy.start()
+        copies.append(copy)
+    bias_in[at_chol] = bias_ref[...]
+    for copy in copies:
+        copy.wait()
+    force = bias_in[0]
+    for c in range(1, chol):
+        force = force + bias_in[c]
+    force_ref[...] = force
+    field = (noise_ref[...] - SQRT_TAU * force).astype(bf16)
+    coeff = jnp.dot(field, hot_ref[...], preferred_element_type=f32)
+    sent[...] = jnp.concatenate([coeff, place_ref[...]], axis=0).astype(bf16)
+    copies = []
+    for j, peer in enumerate(in_wide):
+        copy = pltpu.make_async_remote_copy(
+            src_ref=sent,
+            dst_ref=got_in.at[at_wide],
+            send_sem=got_send.at[j],
+            recv_sem=got_recv.at[j],
+            device_id=peer,
+            device_id_type=mesh_id,
+        )
+        copy.start()
+        copies.append(copy)
+    got_in[at_wide] = sent[...]
+    for copy in copies:
+        copy.wait()
+    got_ref[...] = got_in[...]
+
+
+def share(bias_part, aux_noise, hot, places, chol, wide):
+    bf16 = jnp.bfloat16
+    slots = hot.shape[1]
+    rows = bias_part.shape[0] + places.shape[0]
+    return pl.pallas_call(
+        functools.partial(share_kernel, chol, wide),
+        out_shape=(
+            jax.ShapeDtypeStruct(bias_part.shape, jnp.float32),
+            jax.ShapeDtypeStruct((wide, rows, slots), bf16),
+        ),
+        in_specs=[pl.BlockSpec(memory_space=pltpu.VMEM)] * 4,
+        out_specs=(pl.BlockSpec(memory_space=pltpu.VMEM),) * 2,
+        scratch_shapes=[
+            pltpu.VMEM((chol,) + bias_part.shape, jnp.float32),
+            pltpu.VMEM((wide, rows, slots), bf16),
+            pltpu.VMEM((rows, slots), bf16),
+            pltpu.SemaphoreType.DMA((chol - 1,)),
+            pltpu.SemaphoreType.DMA((chol - 1,)),
+            pltpu.SemaphoreType.DMA((wide - 1,)),
+            pltpu.SemaphoreType.DMA((wide - 1,)),
+        ],
+        compiler_params=pltpu.CompilerParams(collective_id=1, has_side_effects=True),
+    )(bias_part, aux_noise, hot, places)
 
 
 def body(
@@ -222,16 +315,18 @@
     going, coming = chol_tiles[:half], chol_tiles[half:]
     parts = [chol_tiles]
     for step in range(1, wide):
-        if step == wide - 1:
-            going, coming, bias_part = lax.optimization_barrier((going, coming, bias_part))
         going = lax.ppermute(going, "wide", right)
         coming = lax.ppermute(coming, "wide", left)
         parts += [going, coming]
-    force_bias = lax.psum(bias_part, "chol")
-    field = (aux_noise - SQRT_TAU * force_bias).astype(bf16)
-    coeff_own = jnp.dot(field, (vec_hot * live[:, None]).T.astype(bf16), preferred_element_type=f32)
-    sent = jnp.concatenate([coeff_own.astype(bf16), place_own.astype(bf16)[None]], axis=0)
-    got = lax.all_gather(sent, "wide", axis=0).astype(f32)
+    force_bias, got = share(
+        bias_part,
+        aux_noise,
+        (vec_hot * live[:, None]).T.astype(bf16),
+        jnp.broadcast_to(place_own.astype(f32)[None], (8, slot_count)),
+        lax.axis_size("chol"),
+        wide,
+    )
+    got = got.astype(f32)
     coeff = lax.dynamic_index_in_dim(got, me * walk_dev, 1, keepdims=False)
     place_all = got[:, walk_all].astype(jnp.int32)
     places = row_blocks * col_blocks

time: 305 us -> 284 us (0.931)
  blocking collectives: 36.1 us -> 0 us
  Pallas kernels: 35.9 us -> 47.9 us
  waiting for transfers between devices: 117 us -> 113 us
    all_gather x1 -> x0, blocking collectives: 30.5 us -> none  [body(): got = lax.all_gather(sent, 'wide', axis=0).astype(f32)]
    pallas_call x0 -> x1, Pallas kernels: none -> 12.2 us  [share(): pl.pallas_call(functools.partial(share_kernel, chol, wide), out_shape=(ja...]
    ppermute x7, waiting for transfers between devices: 7.91 us -> 1.33 us  [body(): coming = lax.ppermute(coming, 'wide', left)]
    psum x1 -> x0, blocking collectives: 5.63 us -> none  [body(): force_bias = lax.psum(bias_part, 'chol')]
    unnamed x33 -> x28, local copies, waits for them, and re-layouts: 38.3 us -> 40.3 us
  transfers between devices with their start and end apart: 16 -> 16, of which waited for: 13 -> 7; matrix products, arithmetic and copies ran while one was open for 23% -> 26% of each run, Pallas kernels for 0% -> 4%
where the time goes in v4:
time: 284 us; the launch traced here: 283 us
  waiting for transfers between devices  113 us (40%)
  local copies, waits for them, and re-layouts  53.2 us (19%)
  Pallas kernels  47.9 us (17%)
  matrix products  30.2 us (11%)
  starting transfers between devices  20.6 us (7%)
  between operations  14.9 us (5%)
  other arithmetic  3.16 us (1%)
    ppermute x7, waiting for transfers between devices, body(): going = lax.ppermute(going, 'wide', right)  111 us
    unnamed x28, local copies, waits for them, and re-layouts  40.3 us
    pallas_call x1, Pallas kernels, taylor(): pl.pallas_call(functools.partial(series_kernel, pairs), out_shape=jax.Sha...  35.6 us
    ppermute x7, starting transfers between devices, body(): going = lax.ppermute(going, 'wide', right)  16.7 us
    pallas_call x1, Pallas kernels, share(): pl.pallas_call(functools.partial(share_kernel, chol, wide), out_shape=(ja...  12.2 us
    dot_general x1, matrix products, body(): jnp.einsum('akt,tpq->apkq', weights_in.reshape(row_blocks, col_blocks, -1...  8.88 us
    dot_general x1, matrix products, body(): jnp.einsum('tqn,wcqn->wtc', projected, theta_blocks, preferred_element_ty...  6.41 us
  transfers between devices with their start and end apart: 16, of which 7 were waited for; matrix products, arithmetic and copies ran while one was open for 26% of the time, Pallas kernels for 4%

profile of v4, /device:TPU:0, one launch (start us, length us, event | category | flops | bytes accessed | tf_op | source)
XLA Modules:
  0.0 283.0 jit_solution(13429659803362789018)
XLA Ops:
  7.2 0.7 all-gather.5.cloned.1.call-update
  8.0 1.7 fusion.47
  9.6 1.7 copy.94
  11.3 3.0 %collective-permute-start = (bf16[32,128,128]{2,0,1:T(8,128)(2,1)}, bf16[32,128,128]{2,0,1:T(8,128)(2,1)}, u32[]{:S(2)}, u32[]{:S(2)}) collective-permute-start(bf16[32,128,128]{2,0,1:T(8,128)(2,1)} %copy.94), channel_id=1, source_target_pairs={{0,8},{8,16},{16,24},{24,28},{28,20},{20,12},{12,4},{4,0},{1,9},{9... | collective-permute-start | bytes 3145736 | tf_op jit(solution)/shard_map/ppermute | solution.py:318
  14.3 0.7 copy.95
  15.1 29.0 %collective-permute-done = bf16[32,128,128]{2,0,1:T(8,128)(2,1)} collective-permute-done((bf16[32,128,128]{2,0,1:T(8,128)(2,1)}, bf16[32,128,128]{2,0,1:T(8,128)(2,1)}, u32[]{:S(2)}, u32[]{:S(2)}) %collective-permute-start) | collective-permute-done | bytes 1048608 | tf_op jit(solution)/shard_map/ppermute | solution.py:318
  44.1 2.5 collective-permute-start.2
  46.6 0.7 add_convert_fusion
  47.2 0.7 fusion.44
  47.9 0.7 fusion.45
  48.6 1.6 reshape.111
  50.9 3.9 %convolution_convert_fusion = bf16[64,32768]{1,0:T(8,128)(2,1)} fusion(bf16[16,32768]{1,0:T(8,128)(2,1)S(1)} %reshape.111, s32[64]{0:T(128)} %param.16), kind=kOutput, calls=%fused_computation | convolution fusion | flops 69209088 | bytes 5243136 | tf_op jit(solution)/shard_map/dot_general | solution.py:305
  54.8 23.6 %collective-permute-done.2 = bf16[32,128,128]{2,0,1:T(8,128)(2,1)} collective-permute-done((bf16[32,128,128]{2,0,1:T(8,128)(2,1)}, bf16[32,128,128]{2,0,1:T(8,128)(2,1)}, u32[]{:S(2)}, u32[]{:S(2)}) %collective-permute-start.2) | collective-permute-done | bytes 1048608 | tf_op jit(solution)/shard_map/ppermute | solution.py:318
  78.4 2.5 collective-permute-start.4
  80.9 3.3 %copy.68 = bf16[8,8,128,256]{3,2,1,0:T(8,128)(2,1)S(1)} copy(bf16[8,8,128,256]{3,1,2,0:T(8,128)(2,1)} %bitcast.69) | data formatting | bytes 8388608
  84.2 0.6 select_convert_fusion.1.hot_ref
  84.9 2.7 constant_dynamic-update-slice_fusion.14
  87.5 3.3 %convert_bitcast_fusion = bf16[64,128,256]{1,2,0:T(8,128)(2,1)} fusion(bf16[64,128,256]{2,1,0:T(8,128)(2,1)S(1)} %bitcast.70, bf16[64,128,128]{2,1,0:T(8,128)(2,1)S(1)} %copy-done), kind=kOutput, calls=%fused_computation.6 | convolution fusion | flops 538968064 | bytes 10485760 | tf_op jit(solution)/shard_map/tpq,tpn->tqn/dot_general | solution.py:307
  90.8 26.6 %collective-permute-done.4 = bf16[32,128,128]{2,0,1:T(8,128)(2,1)} collective-permute-done((bf16[32,128,128]{2,0,1:T(8,128)(2,1)}, bf16[32,128,128]{2,0,1:T(8,128)(2,1)}, u32[]{:S(2)}, u32[]{:S(2)}) %collective-permute-start.4) | collective-permute-done | bytes 1048608 | tf_op jit(solution)/shard_map/ppermute | solution.py:318
  117.4 4.1 %collective-permute-start.6 = (bf16[32,128,128]{2,0,1:T(8,128)(2,1)}, bf16[32,128,128]{2,0,1:T(8,128)(2,1)}, u32[]{:S(2)}, u32[]{:S(2)}) collective-permute-start(bf16[32,128,128]{2,0,1:T(8,128)(2,1)} %collective-permute-done.4), channel_id=1, source_target_pairs={{0,8},{8,16},{16,24},{24,28},{28,20},{20,12},{12,4},{4,0},{1,9},{9... | collective-permute-start | bytes 3145736 | tf_op jit(solution)/shard_map/ppermute | solution.py:318
  121.5 2.4 constant_dynamic-update-slice_fusion.13
  123.9 2.4 constant_dynamic-update-slice_fusion.12
  126.3 1.1 collective-permute-start.7
  127.3 1.9 convolution_convert_fusion.1
  129.3 2.4 constant_dynamic-update-slice_fusion.11
  131.7 2.4 constant_dynamic-update-slice_fusion.10
  134.1 2.4 constant_dynamic-update-slice_fusion.9
  136.5 2.4 constant_dynamic-update-slice_fusion.8
  138.9 4.1 %collective-permute-done.6 = bf16[32,128,128]{2,0,1:T(8,128)(2,1)} collective-permute-done((bf16[32,128,128]{2,0,1:T(8,128)(2,1)}, bf16[32,128,128]{2,0,1:T(8,128)(2,1)}, u32[]{:S(2)}, u32[]{:S(2)}) %collective-permute-start.6) | collective-permute-done | bytes 1048608 | tf_op jit(solution)/shard_map/ppermute | solution.py:318
  143.0 2.0 collective-permute-start.8
  145.0 2.9 %fusion.9 = bf16[8,512,256]{2,0,1:T(8,128)(2,1)S(1)} fusion(bf16[8,512,256]{2,1,0:T(8,128)(2,1)} %all-gather.3.cloned.1.call-done, s32[8]{0:T(128)S(1)} %copy-done.2), kind=kOutput, calls=%fused_computation.13 | convolution fusion | flops 17825856 | bytes 4194336 | tf_op jit(solution)/shard_map/jw,wmn->jmn/dot_general | solution.py:294
  147.9 1.3 collective-permute-done.7
  149.2 1.2 collective-permute-start.9
  150.4 2.1 fusion.12
  152.5 4.3 %copy.53 = bf16[8,4,128,256]{2,0,3,1:T(8,128)(2,1)} copy(bf16[8,4,128,256]{3,2,1,0:T(8,128)(2,1)} %bitcast.72) | data formatting | bytes 4194304 | tf_op jit(solution)/shard_map/reshape | solution.py:310
  156.8 6.4 %fusion.23 = f32[8,64]{1,0:T(8,128)S(1)} fusion(bf16[8,4,128,256]{2,0,3,1:T(8,128)(2,1)} %copy.53, bf16[64,128,256]{1,2,0:T(8,128)(2,1)} %convert_bitcast_fusion, f32[64,4]{0,1:T(4,128)S(1)} %fusion.44), kind=kOutput, calls=%fused_computation.18 | convolution fusion | flops 134221312 | bytes 6294528 | tf_op jit(solution)/shard_map/tqn,wcqn->wtc/dot_general | solution.py:311
  163.2 0.8 fusion.34.bias_ref
  164.0 0.6 broadcast_in_dim.50.place_ref
  164.6 12.2 %shard_map.122 = (f32[8,64]{1,0:T(8,128)}, bf16[8,16,64]{2,1,0:T(8,128)(2,1)}) custom-call(f32[8,64]{1,0:T(8,128)} %fusion.34.bias_ref, f32[8,64]{1,0:T(8,128)} %noise_ref.1, bf16[64,64]{1,0:T(8,128)(2,1)} %select_convert_fusion.1.hot_ref, f32[8,64]{1,0:T(8,128)} %broadcast_in_dim.50.place_ref), custom_call_target="tpu_custom_call" | custom-call | tf_op jit(solution)/shard_map/pallas_call | solution.py:235
  176.8 0.8 convert_element_type.85
  177.6 1.3 collective-permute-start.10
  179.0 0.8 collective-permute-start.11
  180.4 0.5 constant_dynamic-slice_fusion
  180.9 0.7 copy.61
  181.6 0.2 copy.62
  181.8 20.7 %collective-permute-done.10 = bf16[32,128,128]{2,0,1:T(8,128)(2,1)} collective-permute-done((bf16[32,128,128]{2,0,1:T(8,128)(2,1)}, bf16[32,128,128]{2,0,1:T(8,128)(2,1)}, u32[]{:S(2)}, u32[]{:S(2)}) %collective-permute-start.10) | collective-permute-done | bytes 1048608 | tf_op jit(solution)/shard_map/ppermute | solution.py:318
  202.5 1.3 collective-permute-start.12
  203.9 0.7 collective-permute-start.13
  204.7 2.4 constant_dynamic-update-slice_fusion.7
  207.1 2.4 constant_dynamic-update-slice_fusion.6
  209.5 2.4 constant_dynamic-update-slice_fusion.5
  211.9 2.4 constant_dynamic-update-slice_fusion.4
  214.3 2.5 constant_dynamic-update-slice_fusion.3
  216.8 2.4 constant_dynamic-update-slice_fusion.2
  219.2 7.0 %collective-permute-done.12 = bf16[32,128,128]{2,0,1:T(8,128)(2,1)S(1)} collective-permute-done((bf16[32,128,128]{2,0,1:T(8,128)(2,1)}, bf16[32,128,128]{2,0,1:T(8,128)(2,1)S(1)}, u32[]{:S(2)}, u32[]{:S(2)}) %collective-permute-start.12) | collective-permute-done | bytes 1048608 | tf_op jit(solution)/shard_map/ppermute | solution.py:318
  226.3 1.2 constant_dynamic-update-slice_fusion.1
  227.5 1.2 constant_dynamic-update-slice_fusion
  228.7 8.9 %convert_bitcast_fusion.1 = bf16[16,128,4,128]{3,0,2,1:T(8,128)(2,1)S(1)} fusion(bf16[512,128,128]{2,0,1:T(8,128)(2,1)} %constant_dynamic-update-slice_fusion, bf16[512]{0:T(512)(128)(2,1)S(1)} %pad_maximum_fusion.1, s32[16,4]{0,1:T(4,128)S(1)} %multiply_add_fusion, s32[512]{0:T(512)S(1)} %pad_add_fusion.1), kind=kOutput, calls=%fused_computation.12 | convolution fusion | flops 1074855936 | bytes 18877696 | tf_op jit(solution)/shard_map/akt,tpq->apkq/dot_general | solution.py:352
  237.6 1.0 copy.60
  238.6 0.4 copy.96
  238.9 35.6 %shard_map.123 = bf16[2,512,128]{2,1,0:T(8,128)(2,1)S(1)} custom-call(bf16[2048,512]{1,0:T(8,128)(2,1)S(1)} %bitcast.66, bf16[2,512,128]{2,1,0:T(8,128)(2,1)S(1)} %bitcast.67), custom_call_target="tpu_custom_call" | custom-call | tf_op jit(solution)/shard_map/pallas_call | solution.py:137
  274.6 0.1 copy.63
  274.7 0.8 copy.64
  275.6 0.6 copy.113
  (43 shorter events, 1.1 us)
Async XLA Ops:
  7.2 77.7 %copy-start = (bf16[64,128,128]{2,1,0:T(8,128)(2,1)S(1)}, bf16[64,128,128]{2,1,0:T(8,128)(2,1)}, u32[]{:S(2)}) copy-start(bf16[64,128,128]{2,1,0:T(8,128)(2,1)} %param.14) | copy-start | bytes 6291460
  7.2 77.0 %copy-start.3 = (s32[64]{0:T(128)S(1)}, s32[64]{0:T(128)}, u32[]{:S(2)}) copy-start(s32[64]{0:T(128)} %param.15) | copy-start | bytes 772
  7.2 120.2 %all-gather.5.cloned.1.call-start = ((), (), s32[]{:S(2)}) async-start(), calls=%async_computation.1 | async-start | bytes 1179648 | tf_op jit(solution)/shard_map/all_gather | solution.py:282
  7.9 137.1 %all-gather.3.cloned.1.call-start = ((), (), s32[]{:S(2)}) async-start(), calls=%async_computation | async-start | bytes 2359296 | tf_op jit(solution)/shard_map/all_gather | solution.py:281
  11.3 32.8 %collective-permute-start = (bf16[32,128,128]{2,0,1:T(8,128)(2,1)}, bf16[32,128,128]{2,0,1:T(8,128)(2,1)}, u32[]{:S(2)}, u32[]{:S(2)}) collective-permute-start(bf16[32,128,128]{2,0,1:T(8,128)(2,1)} %copy.94), channel_id=1, source_target_pairs={{0,8},{8,16},{16,24},{24,28},{28,20},{20,12},{12,4},{4,0},{1,9},{9... | collective-permute-start | bytes 3145736 | tf_op jit(solution)/shard_map/ppermute | solution.py:318
  15.0 32.9 %collective-permute-start.1 = (bf16[32,128,128]{2,0,1:T(8,128)(2,1)S(1)}, bf16[32,128,128]{2,0,1:T(8,128)(2,1)}, u32[]{:S(2)}, u32[]{:S(2)}) collective-permute-start(bf16[32,128,128]{2,0,1:T(8,128)(2,1)S(1)} %copy.95), channel_id=1, source_target_pairs={{8,0},{16,8},{24,16},{28,24},{20,28},{12,20},{4,12},{0,4},{9,1},{1... | collective-permute-start | bytes 3145736 | tf_op jit(solution)/shard_map/ppermute | solution.py:319
  44.1 34.3 %collective-permute-start.2 = (bf16[32,128,128]{2,0,1:T(8,128)(2,1)}, bf16[32,128,128]{2,0,1:T(8,128)(2,1)}, u32[]{:S(2)}, u32[]{:S(2)}) collective-permute-start(bf16[32,128,128]{2,0,1:T(8,128)(2,1)} %collective-permute-done), channel_id=1, source_target_pairs={{0,8},{8,16},{16,24},{24,28},{28,20},{20,12},{12,4},{4,0},{1,9},{9... | collective-permute-start | bytes 3145736 | tf_op jit(solution)/shard_map/ppermute | solution.py:318
  47.9 36.9 %collective-permute-start.3 = (bf16[32,128,128]{2,0,1:T(8,128)(2,1)}, bf16[32,128,128]{2,0,1:T(8,128)(2,1)}, u32[]{:S(2)}, u32[]{:S(2)}) collective-permute-start(bf16[32,128,128]{2,0,1:T(8,128)(2,1)} %collective-permute-done.1), channel_id=1, source_target_pairs={{8,0},{16,8},{24,16},{28,24},{20,28},{12,20},{4,12},{0,4},{9,1},{1... | collective-permute-start | bytes 3145736 | tf_op jit(solution)/shard_map/ppermute | solution.py:319
  50.2 77.2 %copy-start.2 = (s32[8]{0:T(128)S(1)}, s32[8]{0:T(128)}, u32[]{:S(2)}) copy-start(s32[8]{0:T(128)} %param.19) | copy-start | bytes 100
  78.4 38.9 %collective-permute-start.4 = (bf16[32,128,128]{2,0,1:T(8,128)(2,1)}, bf16[32,128,128]{2,0,1:T(8,128)(2,1)}, u32[]{:S(2)}, u32[]{:S(2)}) collective-permute-start(bf16[32,128,128]{2,0,1:T(8,128)(2,1)} %collective-permute-done.2), channel_id=1, source_target_pairs={{0,8},{8,16},{16,24},{24,28},{28,20},{20,12},{12,4},{4,0},{1,9},{9... | collective-permute-start | bytes 3145736 | tf_op jit(solution)/shard_map/ppermute | solution.py:318
  84.8 41.4 %collective-permute-start.5 = (bf16[32,128,128]{2,0,1:T(8,128)(2,1)}, bf16[32,128,128]{2,0,1:T(8,128)(2,1)}, u32[]{:S(2)}, u32[]{:S(2)}) collective-permute-start(bf16[32,128,128]{2,0,1:T(8,128)(2,1)} %collective-permute-done.3), channel_id=1, source_target_pairs={{8,0},{16,8},{24,16},{28,24},{20,28},{12,20},{4,12},{0,4},{9,1},{1... | collective-permute-start | bytes 3145736 | tf_op jit(solution)/shard_map/ppermute | solution.py:319
  117.4 25.6 %collective-permute-start.6 = (bf16[32,128,128]{2,0,1:T(8,128)(2,1)}, bf16[32,128,128]{2,0,1:T(8,128)(2,1)}, u32[]{:S(2)}, u32[]{:S(2)}) collective-permute-start(bf16[32,128,128]{2,0,1:T(8,128)(2,1)} %collective-permute-done.4), channel_id=1, source_target_pairs={{0,8},{8,16},{16,24},{24,28},{28,20},{20,12},{12,4},{4,0},{1,9},{9... | collective-permute-start | bytes 3145736 | tf_op jit(solution)/shard_map/ppermute | solution.py:318
  126.3 23.0 %collective-permute-start.7 = (bf16[32,128,128]{2,0,1:T(8,128)(2,1)}, bf16[32,128,128]{2,0,1:T(8,128)(2,1)}, u32[]{:S(2)}, u32[]{:S(2)}) collective-permute-start(bf16[32,128,128]{2,0,1:T(8,128)(2,1)} %collective-permute-done.5), channel_id=1, source_target_pairs={{8,0},{16,8},{24,16},{28,24},{20,28},{12,20},{4,12},{0,4},{9,1},{1... | collective-permute-start | bytes 3145736 | tf_op jit(solution)/shard_map/ppermute | solution.py:319
  143.0 34.6 %collective-permute-start.8 = (bf16[32,128,128]{2,0,1:T(8,128)(2,1)}, bf16[32,128,128]{2,0,1:T(8,128)(2,1)}, u32[]{:S(2)}, u32[]{:S(2)}) collective-permute-start(bf16[32,128,128]{2,0,1:T(8,128)(2,1)} %collective-permute-done.6), channel_id=1, source_target_pairs={{0,8},{8,16},{16,24},{24,28},{28,20},{20,12},{12,4},{4,0},{1,9},{9... | collective-permute-start | bytes 3145736 | tf_op jit(solution)/shard_map/ppermute | solution.py:318
  149.2 29.8 %collective-permute-start.9 = (bf16[32,128,128]{2,0,1:T(8,128)(2,1)}, bf16[32,128,128]{2,0,1:T(8,128)(2,1)}, u32[]{:S(2)}, u32[]{:S(2)}) collective-permute-start(bf16[32,128,128]{2,0,1:T(8,128)(2,1)} %collective-permute-done.7), channel_id=1, source_target_pairs={{8,0},{16,8},{24,16},{28,24},{20,28},{12,20},{4,12},{0,4},{9,1},{1... | collective-permute-start | bytes 3145736 | tf_op jit(solution)/shard_map/ppermute | solution.py:319
  177.6 24.9 %collective-permute-start.10 = (bf16[32,128,128]{2,0,1:T(8,128)(2,1)}, bf16[32,128,128]{2,0,1:T(8,128)(2,1)}, u32[]{:S(2)}, u32[]{:S(2)}) collective-permute-start(bf16[32,128,128]{2,0,1:T(8,128)(2,1)} %collective-permute-done.8), channel_id=1, source_target_pairs={{0,8},{8,16},{16,24},{24,28},{28,20},{20,12},{12,4},{4,0},{1,9},{9... | collective-permute-start | bytes 3145736 | tf_op jit(solution)/shard_map/ppermute | solution.py:318
  179.0 24.9 %collective-permute-start.11 = (bf16[32,128,128]{2,0,1:T(8,128)(2,1)}, bf16[32,128,128]{2,0,1:T(8,128)(2,1)}, u32[]{:S(2)}, u32[]{:S(2)}) collective-permute-start(bf16[32,128,128]{2,0,1:T(8,128)(2,1)} %collective-permute-done.9), channel_id=1, source_target_pairs={{8,0},{16,8},{24,16},{28,24},{20,28},{12,20},{4,12},{0,4},{9,1},{1... | collective-permute-start | bytes 3145736 | tf_op jit(solution)/shard_map/ppermute | solution.py:319
  202.5 23.8 %collective-permute-start.12 = (bf16[32,128,128]{2,0,1:T(8,128)(2,1)}, bf16[32,128,128]{2,0,1:T(8,128)(2,1)S(1)}, u32[]{:S(2)}, u32[]{:S(2)}) collective-permute-start(bf16[32,128,128]{2,0,1:T(8,128)(2,1)} %collective-permute-done.10), channel_id=1, source_target_pairs={{0,8},{8,16},{16,24},{24,28},{28,20},{20,12},{12,4},{4,0},{1,9},{9... | collective-permute-start | bytes 3145736 | tf_op jit(solution)/shard_map/ppermute | solution.py:318
  203.9 23.6 %collective-permute-start.13 = (bf16[32,128,128]{2,0,1:T(8,128)(2,1)}, bf16[32,128,128]{2,0,1:T(8,128)(2,1)S(1)}, u32[]{:S(2)}, u32[]{:S(2)}) collective-permute-start(bf16[32,128,128]{2,0,1:T(8,128)(2,1)} %collective-permute-done.11), channel_id=1, source_target_pairs={{8,0},{16,8},{24,16},{28,24},{20,28},{12,20},{4,12},{0,4},{9,1},{1... | collective-permute-start | bytes 3145736 | tf_op jit(solution)/shard_map/ppermute | solution.py:319
  228.7 46.9 %copy-start.1 = (f32[8,64]{1,0:T(8,128)S(1)}, f32[8,64]{1,0:T(8,128)}, u32[]{:S(2)}) copy-start(f32[8,64]{1,0:T(8,128)} %get-tuple-element.18) | copy-start | bytes 6148
Sparse Core Ops, SparseCore 0:
  10.1 46.3 all-gather.4
  58.7 62.2 all-gather.2
